TPU v7x, 512 devices: a whole 4x4x16 slice. The times are simulated.
512 devices in a mesh: shots: 128 (over z, y, core), sub: 4 (over x).
Axes of the slice: x: 4, y: 4, z: 16, core: 2. Of those that a mesh axis runs over, the one named last changes fastest.
Arguments:
- model: float32 [128, 512, 256], P('shots'), may hold values from 0.08 to 0.19
- anchor_x: int32 [128], replicated, may hold values from 0 to 496
- anchor_y: int32 [128], replicated, may hold values from 0 to 128
- state_before: bfloat16 [128, 128, 16, 128], P('shots', None, 'sub'), may hold values from -1.5 to 1.5
- state_now: bfloat16 [128, 128, 16, 128], P('shots', None, 'sub'), may hold values from -1.5 to 1.5
- adjoint_later: bfloat16 [128, 128, 16, 128], P('shots', None, 'sub'), may hold values from -1.5 to 1.5
- adjoint_latest: bfloat16 [128, 128, 16, 128], P('shots', None, 'sub'), may hold values from -1.5 to 1.5
- wavelet: float32 [128, 3], P('shots'), may hold values from -8 to 8
- src_index: int32 [128], P('shots'), may hold values from 0 to 262143
- rec_index: int32 [128, 512], P('shots'), may hold values from 0 to 262143
- observed: float32 [128, 3, 512], P('shots'), may hold values from -3 to 3
Outputs:
- gradient: float32 [128, 512, 256], P('shots', 'sub')
- adjoint_first: bfloat16 [128, 128, 16, 128], P('shots', None, 'sub')
- adjoint_second: bfloat16 [128, 128, 16, 128], P('shots', None, 'sub')
All inputs are finite; a program needn't handle non-finite values.
Results may differ from a plain program's by a relative error of at most 0.001.
Values sent between devices are 32-bit elements; how exact they have to be, the bound alone decides.
No kernel may reach another device: no remote copies, remote signals or barrier semaphores. Data moves between devices by JAX's collectives and lax.ppermute only.
A program may use at most 64 MiB of HBM per device.

v0:
```python
import jax
import jax.numpy as jnp
from jax import lax
from jax.sharding import PartitionSpec as P

STEPS = 3


STENCIL = (-205.0 / 72.0, 8.0 / 5.0, -1.0 / 5.0, 8.0 / 315.0, -1.0 / 560.0)


def with_halo(x, sides, width):
    for axis, dim in sides:
        count, length = (lax.axis_size(axis), x.shape[dim])
        up = [(i, (i + 1) % count) for i in range(count - 1)]
        down = [(j, i) for i, j in up]
        last = lax.slice_in_dim(x, length - width, length, axis=dim)
        leading = lax.slice_in_dim(x, 0, width, axis=dim)
        before = lax.ppermute(last, axis, up)
        after = lax.ppermute(leading, axis, down)
        x = jnp.concatenate([before, x, after], axis=dim)
    return x


def laplace(extended):
    depth = extended.shape[-3]
    inner_x = extended.shape[-2] - 8
    inner_y = extended.shape[-1]
    leading = [(0, 0)] * (extended.ndim - 3)
    padded = jnp.pad(extended, leading + [(4, 4), (0, 0), (4, 4)])

    def window(shift_z, shift_x, shift_y):
        return padded[
            ...,
            4 + shift_z : 4 + shift_z + depth,
            4 + shift_x : 4 + shift_x + inner_x,
            4 + shift_y : 4 + shift_y + inner_y,
        ]

    total = 3.0 * STENCIL[0] * window(0, 0, 0)
    for reach in range(1, 5):
        near = window(reach, 0, 0) + window(-reach, 0, 0)
        near = near + window(0, reach, 0) + window(0, -reach, 0)
        near = near + window(0, 0, reach) + window(0, 0, -reach)
        total = total + STENCIL[reach] * near
    return total


def forward_laplace(field):
    return laplace(with_halo(field, (("sub", 1),), 4))


def locate(flat_index, across, width_x, width_y, row_start):
    cell_z = flat_index // (across * width_y)
    cell_x = flat_index // width_y % across
    cell_y = flat_index % width_y
    inside = (cell_x >= row_start) & (cell_x < row_start + width_x)
    local_x = jnp.clip(cell_x - row_start, 0, width_x - 1)
    return (cell_z, local_x, cell_y, inside)


def per_device(
    model,
    anchor_x,
    anchor_y,
    state_before,
    state_now,
    adjoint_later,
    adjoint_latest,
    wavelet,
    src_index,
    rec_index,
    observed,
):
    groups = lax.axis_size("shots")
    slabs = lax.axis_size("sub")
    depth_rows, model_x, model_y = model.shape
    depth, width_x, width_y = state_now.shape[1:]
    across = width_x * slabs
    row_start = lax.axis_index("sub") * width_x

    def cut_panel(start_x, start_y):
        return lax.dynamic_slice(
            model, (jnp.int32(0), start_x + row_start, start_y), (depth_rows, width_x, width_y)
        )

    panels = jax.vmap(cut_panel)(anchor_x, anchor_y).reshape(groups * depth_rows, width_x, width_y)
    speed = lax.all_to_all(panels, "shots", split_axis=0, concat_axis=0, tiled=True)
    source_z, source_x, source_y, source_in = locate(
        src_index[0], across, width_x, width_y, row_start
    )
    recv_z, recv_x, recv_y, recv_in = locate(rec_index[0], across, width_x, width_y, row_start)
    previous = state_before[0].astype(jnp.float32)
    current = state_now[0].astype(jnp.float32)
    states = [current]
    stored = []
    for index in range(STEPS):
        curvature = forward_laplace(current)
        stored.append(curvature)
        following = 2.0 * current - previous + speed * curvature
        following = following.at[source_z, source_x, source_y].add(
            jnp.where(source_in, wavelet[0, index], 0.0)
        )
        previous, current = (current, following)
        states.append(following)
    adjoint_one = adjoint_later[0].astype(jnp.float32)
    adjoint_two = adjoint_latest[0].astype(jnp.float32)
    shot_grad = jnp.zeros(speed.shape, jnp.float32)
    for index in range(STEPS, 0, -1):
        scaled = speed * adjoint_one
        stacked = jnp.stack([scaled, states[index - 1]])
        both = laplace(with_halo(stacked, (("sub", 2),), 4))
        adjoint_term = both[0]
        earlier_term = both[1]
        adjoint = 2.0 * adjoint_one + adjoint_term - adjoint_two
        sampled = states[index][recv_z, recv_x, recv_y]
        residual = jnp.where(recv_in, sampled - observed[0, index - 1], 0.0)
        adjoint = adjoint.at[recv_z, recv_x, recv_y].add(residual)
        shot_grad = shot_grad + adjoint * earlier_term
        adjoint_two, adjoint_one = (adjoint_one, adjoint)
    returned = lax.all_to_all(shot_grad, "shots", split_axis=0, concat_axis=0, tiled=True).reshape(
        groups, depth_rows, width_x, width_y
    )
    rows = anchor_x[:, None] + row_start + jnp.arange(width_x, dtype=jnp.int32)[None, :]
    columns = anchor_y[:, None] + jnp.arange(width_y, dtype=jnp.int32)[None, :]
    flat_cells = rows[:, :, None] * model_y + columns[:, None, :]
    owned = jnp.zeros((depth_rows, model_x * model_y), jnp.float32)
    owned = owned.at[:, flat_cells].add(jnp.moveaxis(returned, 1, 0))
    owned = owned.reshape(depth_rows, model_x, model_y)
    gradient = lax.psum_scatter(owned, "sub", scatter_dimension=1, tiled=True)
    return (
        gradient,
        adjoint_one.astype(jnp.bfloat16)[None],
        adjoint_two.astype(jnp.bfloat16)[None],
    )


def solution(mesh):
    return jax.shard_map(
        per_device,
        mesh=mesh,
        in_specs=(
            P("shots", None, None),
            P(),
            P(),
            P("shots", None, "sub", None),
            P("shots", None, "sub", None),
            P("shots", None, "sub", None),
            P("shots", None, "sub", None),
            P("shots", None),
            P("shots"),
            P("shots", None),
            P("shots", None, None),
        ),
        out_specs=(
            P("shots", "sub", None),
            P("shots", None, "sub", None),
            P("shots", None, "sub", None),
        ),
        check_vma=False,
    )
```

profile of v0, /device:TPU:24, one launch (start us, length us, event | category | flops | bytes accessed | tf_op | source)
XLA Modules:
  0.0 1162.8 jit_solution(14402947796837247628)
XLA Ops:
  8.6 417.7 %while.4 = (s32[]{:T(128)}, f32[1,512,256]{2,1,0:T(8,128)}, s32[128,3]{0,1:T(4,128)S(1)}, f32[128,1,4,128]{3,2,1,0:T(4,128)}, s32[]{:T(128)}) while((s32[]{:T(128)}, f32[1,512,256]{2,1,0:T(8,128)}, s32[128,3]{0,1:T(4,128)S(1)}, f32[128,1,4,128]{3,2,1,0:T(4,128)}, s32[]{:T(128)}) %tuple.53), condition=%wide.while_cond.3, body=%wide.while_body.3.sunk | while | flops 2 | bytes 5737 | solution.py:83
  9.2 2.7 bitcast_dynamic-update-slice_fusion.2
  25.5 2.7 bitcast_dynamic-update-slice_fusion.2
  38.6 2.7 bitcast_dynamic-update-slice_fusion.2
  48.4 2.7 bitcast_dynamic-update-slice_fusion.2
  54.9 2.7 bitcast_dynamic-update-slice_fusion.2
  81.0 2.7 bitcast_dynamic-update-slice_fusion.2
  87.5 2.7 bitcast_dynamic-update-slice_fusion.2
  103.8 2.7 bitcast_dynamic-update-slice_fusion.2
  110.4 2.7 bitcast_dynamic-update-slice_fusion.2
  120.2 2.7 bitcast_dynamic-update-slice_fusion.2
  136.5 2.7 bitcast_dynamic-update-slice_fusion.2
  143.0 2.7 bitcast_dynamic-update-slice_fusion.2
  152.8 2.7 bitcast_dynamic-update-slice_fusion.2
  156.1 2.7 bitcast_dynamic-update-slice_fusion.2
  159.3 2.7 bitcast_dynamic-update-slice_fusion.2
  162.6 2.7 bitcast_dynamic-update-slice_fusion.2
  169.2 2.7 bitcast_dynamic-update-slice_fusion.2
  172.4 2.7 bitcast_dynamic-update-slice_fusion.2
  185.5 2.7 bitcast_dynamic-update-slice_fusion.2
  192.0 2.7 bitcast_dynamic-update-slice_fusion.2
  208.4 2.7 bitcast_dynamic-update-slice_fusion.2
  218.2 2.7 bitcast_dynamic-update-slice_fusion.2
  224.7 2.7 bitcast_dynamic-update-slice_fusion.2
  241.0 2.7 bitcast_dynamic-update-slice_fusion.2
  260.6 2.7 bitcast_dynamic-update-slice_fusion.2
  276.9 2.7 bitcast_dynamic-update-slice_fusion.2
  309.5 2.7 bitcast_dynamic-update-slice_fusion.2
  316.0 2.7 bitcast_dynamic-update-slice_fusion.2
  325.8 2.7 bitcast_dynamic-update-slice_fusion.2
  335.6 2.7 bitcast_dynamic-update-slice_fusion.2
  361.6 2.7 bitcast_dynamic-update-slice_fusion.2
  368.2 2.7 bitcast_dynamic-update-slice_fusion.2
  378.0 2.7 bitcast_dynamic-update-slice_fusion.2
  384.5 2.7 bitcast_dynamic-update-slice_fusion.2
  387.8 2.7 bitcast_dynamic-update-slice_fusion.2
  413.9 2.7 bitcast_dynamic-update-slice_fusion.2
  426.3 19.3 %all-to-all-start = ((f32[128,4,128]{2,1,0:T(4,128)}), f32[128,4,128]{2,1,0:T(4,128)S(1)}, u32[]{:S(2)}, u32[]{:S(2)}) async-start(f32[128,4,128]{2,1,0:T(4,128)} %bitcast.4), calls=%async_computation | async-start | bytes 524288 | tf_op jit(solution)/shard_map/all_to_all | solution.py:88
  446.6 3.4 collective-permute-start
  456.8 3.2 collective-permute-done.1
  460.5 7.0 all-to-all-done
  471.0 3.4 collective-permute-start.2
  477.0 4.2 gather_fusion.2
  481.3 3.0 collective-permute-done.3
  488.6 3.4 collective-permute-start.6
  493.3 4.2 gather_fusion.1
  498.4 4.6 collective-permute-start.4
  508.8 4.2 gather_fusion
  513.1 3.9 collective-permute-done.5
  517.2 2.9 select_maximum_fusion.6
  523.1 29.8 %scatter_fusion = f32[128,4,128]{2,0,1:T(8,128)S(1)} fusion(f32[128,4,128]{2,0,1:T(8,128)S(1)} %fusion.37, s32[512]{0:T(512)S(1)} %bitcast.131, f32[512]{0:T(512)S(1)} %get-tuple-element.90), kind=kCustom, calls=%fused_computation.3 | custom fusion | flops 512 | bytes 12288 | tf_op jit(solution)/shard_map/scatter-add | solution.py:118
  552.9 3.0 collective-permute-start.8
  557.2 7.3 collective-permute-done.8
  564.5 4.1 collective-permute-done.9
  568.8 2.9 select_maximum_fusion.3
  573.9 29.8 %scatter_fusion.1 = f32[128,4,128]{2,0,1:T(8,128)S(1)} fusion(f32[128,4,128]{2,0,1:T(8,128)S(1)} %convert_subtract_fusion, s32[512]{0:T(512)S(1)} %bitcast.132, f32[512]{0:T(512)S(1)} %get-tuple-element.89), kind=kCustom, calls=%fused_computation.4 | custom fusion | flops 512 | bytes 12288 | tf_op jit(solution)/shard_map/scatter-add | solution.py:118
  608.2 6.1 collective-permute-done.10
  614.3 4.1 collective-permute-done.11
  618.7 2.9 select_maximum_fusion
  623.8 29.8 %scatter_fusion.2 = f32[128,4,128]{2,0,1:T(8,128)S(1)} fusion(f32[128,4,128]{2,0,1:T(8,128)S(1)} %fusion.102, s32[512]{0:T(512)S(1)} %bitcast.133, f32[512]{0:T(512)S(1)} %get-tuple-element.64), kind=kCustom, calls=%fused_computation.5 | custom fusion | flops 512 | bytes 12288 | tf_op jit(solution)/shard_map/scatter-add | solution.py:118
  654.5 7.9 all-to-all-start.1
  662.9 21.5 %all-to-all-done.1 = f32[128,4,128]{2,1,0:T(4,128)S(1)} async-done(((f32[128,4,128]{2,1,0:T(4,128)}), f32[128,4,128]{2,1,0:T(4,128)S(1)}, u32[]{:S(2)}, u32[]{:S(2)}) %all-to-all-start.1) | async-done | bytes 262176 | tf_op jit(solution)/shard_map/all_to_all | solution.py:121
  684.3 451.9 %scatter_custom_fusion.3 = f32[131072]{0:T(1024)S(1)} fusion(s32[65536]{0:T(1024)S(1)} %bitcast.145, f32[65536]{0:T(1024)S(1)} %bitcast.146, f32[]{:T(128)} %constant.153.clone.1), kind=kCustom, calls=%fused_computation.285 | custom fusion | flops 65536 | bytes 524292 | tf_op jit(solution)/shard_map/scatter-add | solution.py:128
  1138.8 17.2 %reduce-scatter.2.cloned.1.call-done = f32[1,128,256]{2,1,0:T(8,128)} async-done(((f32[1,512,256]{2,1,0:T(8,128)}), f32[1,128,256]{2,1,0:T(8,128)}) %reduce-scatter.2.cloned.1.call-update) | async-done | bytes 131088 | tf_op jit(solution)/shard_map/reduce_scatter | solution.py:130
  (434 shorter events, 358.5 us)
Async XLA Ops:
  7.2 460.4 %copy-start.7 = (bf16[1,128,4,128]{3,2,1,0:T(4,128)(2,1)S(1)}, bf16[1,128,4,128]{3,2,1,0:T(4,128)(2,1)}, u32[]{:S(2)}) copy-start(bf16[1,128,4,128]{3,2,1,0:T(4,128)(2,1)} %param.20) | copy-start | bytes 393220
  426.3 41.2 %all-to-all-start = ((f32[128,4,128]{2,1,0:T(4,128)}), f32[128,4,128]{2,1,0:T(4,128)S(1)}, u32[]{:S(2)}, u32[]{:S(2)}) async-start(f32[128,4,128]{2,1,0:T(4,128)} %bitcast.4), calls=%async_computation | async-start | bytes 524288 | tf_op jit(solution)/shard_map/all_to_all | solution.py:88
  446.6 10.2 collective-permute-start
  450.0 10.0 collective-permute-start.1
  460.5 15.2 %copy-start.10 = (f32[1,3,512]{2,0,1:T(1,128)S(1)}, f32[1,3,512]{2,0,1:T(1,128)}, u32[]{:S(2)}) copy-start(f32[1,3,512]{2,0,1:T(1,128)} %param.27) | copy-start | bytes 18436
  460.5 20.8 %copy-start.2 = (bf16[1,128,4,128]{3,2,1,0:T(4,128)(2,1)S(1)}, bf16[1,128,4,128]{3,2,1,0:T(4,128)(2,1)}, u32[]{:S(2)}) copy-start(bf16[1,128,4,128]{3,2,1,0:T(4,128)(2,1)} %param.22) | copy-start | bytes 393220
  468.6 16.2 %copy-start.5 = (bf16[1,128,4,128]{3,2,1,0:T(4,128)(2,1)S(1)}, bf16[1,128,4,128]{3,2,1,0:T(4,128)(2,1)}, u32[]{:S(2)}) copy-start(bf16[1,128,4,128]{3,2,1,0:T(4,128)(2,1)} %param.21) | copy-start | bytes 393220
  471.0 10.3 collective-permute-start.2
  474.4 9.9 collective-permute-start.3
  484.9 8.4 copy-start.9
  488.6 15.7 %collective-permute-start.6 = (f32[128,4,128]{2,0,1:T(8,128)S(1)}, f32[128,4,128]{2,0,1:T(8,128)S(1)}, u32[]{:S(2)}, u32[]{:S(2)}) collective-permute-start(f32[128,4,128]{2,0,1:T(8,128)S(1)} %scatter-add.44), channel_id=1, source_target_pairs={{0,1},{1,2},{2,3},{4,5},{5,6},{6,7},{8,9},{9,10},{10,11},{12,13},{... | collective-permute-start | bytes 786440 | tf_op jit(solution)/shard_map/ppermute | solution.py:19
  492.0 12.3 %collective-permute-start.7 = (f32[128,4,128]{2,0,1:T(8,128)S(1)}, f32[128,4,128]{2,0,1:T(8,128)S(1)}, u32[]{:S(2)}, u32[]{:S(2)}) collective-permute-start(f32[128,4,128]{2,0,1:T(8,128)S(1)} %scatter-add.44), channel_id=1, source_target_pairs={{1,0},{2,1},{3,2},{5,4},{6,5},{7,6},{9,8},{10,9},{11,10},{13,12},{... | collective-permute-start | bytes 786440 | tf_op jit(solution)/shard_map/ppermute | solution.py:20
  498.4 14.7 %collective-permute-start.4 = (f32[2,128,4,128]{3,1,2,0:T(8,128)}, f32[2,128,4,128]{3,1,2,0:T(8,128)S(1)}, u32[]{:S(2)}, u32[]{:S(2)}) collective-permute-start(f32[2,128,4,128]{3,1,2,0:T(8,128)} %pad_maximum_fusion.3), channel_id=1, source_target_pairs={{0,1},{1,2},{2,3},{4,5},{5,6},{6,7},{8,9},{9,10},{10,11},{12,13},{... | collective-permute-start | bytes 1572872 | tf_op jit(solution)/shard_map/ppermute | solution.py:19
  503.0 14.1 %collective-permute-start.5 = (f32[2,128,4,128]{3,1,2,0:T(8,128)}, f32[2,128,4,128]{3,1,2,0:T(8,128)S(1)}, u32[]{:S(2)}, u32[]{:S(2)}) collective-permute-start(f32[2,128,4,128]{3,1,2,0:T(8,128)} %pad_maximum_fusion.3), channel_id=1, source_target_pairs={{1,0},{2,1},{3,2},{5,4},{6,5},{7,6},{9,8},{10,9},{11,10},{13,12},{... | collective-permute-start | bytes 1572872 | tf_op jit(solution)/shard_map/ppermute | solution.py:20
  520.1 2.1 copy-start.3
  520.1 2.1 copy-start.8
  522.2 0.8 copy-start
  552.9 11.6 collective-permute-start.8
  555.9 12.7 %collective-permute-start.9 = (f32[2,128,4,128]{3,1,2,0:T(8,128)S(1)}, f32[2,128,4,128]{3,1,2,0:T(8,128)S(1)}, u32[]{:S(2)}, u32[]{:S(2)}) collective-permute-start(f32[2,128,4,128]{3,1,2,0:T(8,128)S(1)} %pad_maximum_fusion.4), channel_id=1, source_target_pairs={{1,0},{2,1},{3,2},{5,4},{6,5},{7,6},{9,8},{10,9},{11,10},{13,12},{... | collective-permute-start | bytes 1572872 | tf_op jit(solution)/shard_map/ppermute | solution.py:20
  571.7 2.1 copy-start.4
  604.4 9.9 collective-permute-start.10
  606.7 11.8 %collective-permute-start.11 = (f32[2,128,4,128]{3,1,2,0:T(8,128)S(1)}, f32[2,128,4,128]{3,1,2,0:T(8,128)S(1)}, u32[]{:S(2)}, u32[]{:S(2)}) collective-permute-start(f32[2,128,4,128]{3,1,2,0:T(8,128)S(1)} %pad_maximum_fusion.5), channel_id=1, source_target_pairs={{1,0},{2,1},{3,2},{5,4},{6,5},{7,6},{9,8},{10,9},{11,10},{13,12},{... | collective-permute-start | bytes 1572872 | tf_op jit(solution)/shard_map/ppermute | solution.py:20
  623.7 29.8 %copy-start.1 = (f32[2,128,4,128]{3,1,2,0:T(8,128)S(1)}, f32[2,128,4,128]{3,1,2,0:T(8,128)}, u32[]{:S(2)}) copy-start(f32[2,128,4,128]{3,1,2,0:T(8,128)} %copy-done) | copy-start | bytes 1572868
  623.7 38.7 %copy-start.11 = (s32[128]{0:T(128)S(1)}, s32[128]{0:T(128)}, u32[]{:S(2)}) copy-start(s32[128]{0:T(128)} %param.19) | copy-start | bytes 1540
  653.5 483.7 %copy-start.6 = (bf16[1,128,4,128]{3,1,2,0:T(8,128)(2,1)S(1)}, bf16[1,128,4,128]{3,1,2,0:T(8,128)(2,1)}, u32[]{:S(2)}) copy-start(bf16[1,128,4,128]{3,1,2,0:T(8,128)(2,1)} %get-tuple-element.78) | copy-start | bytes 393220
  654.5 29.8 %all-to-all-start.1 = ((f32[128,4,128]{2,1,0:T(4,128)}), f32[128,4,128]{2,1,0:T(4,128)S(1)}, u32[]{:S(2)}, u32[]{:S(2)}) async-start(f32[128,4,128]{2,1,0:T(4,128)} %copy.39), calls=%async_computation.1 | async-start | bytes 524288 | tf_op jit(solution)/shard_map/all_to_all | solution.py:121
  662.4 493.6 %reduce-scatter.2.cloned.1.call-start = ((), (), s32[]{:S(2)}) async-start(), calls=%async_computation.3 | async-start | bytes 655360 | tf_op jit(solution)/shard_map/reduce_scatter | solution.py:130
Sparse Core Ops, SparseCore 0:
  1137.4 18.5 reduce-scatter.1
where the time goes:
time: 1180 us; the launch traced here: 1160 us
  other arithmetic  569 us (48%)
  local copies, waits for them, and re-layouts  438 us (37%)
  waiting for transfers between devices  77.5 us (7%)
  starting transfers between devices  55.2 us (5%)
  between operations  22.6 us (2%)
    scatter-add x1, other arithmetic, per_device(): owned = owned.at[:, flat_cells].add(jnp.moveaxis(returned, 1, 0))  452 us
    gather x384, local copies, waits for them, and re-layouts  418 us
    scatter-add x3, other arithmetic, per_device(): adjoint = adjoint.at[recv_z, recv_x, recv_y].add(residual)  89.3 us
  transfers between devices with their start and end apart: 15, of which 10 were waited for; matrix products, arithmetic and copies ran while one was open for 2% of the time, Pallas kernels for 0%

commit v1 on v0

v1 whole, which is shorter than its diff:
```python
import functools

import jax
import jax.numpy as jnp
import numpy as np
from jax import lax
from jax.experimental import pallas as pl
from jax.experimental.pallas import tpu as pltpu
from jax.sharding import PartitionSpec as P

STEPS = 3
REACH = 4
UNIT = 5040.0
WHOLE = (8064.0, -1008.0, 128.0, -9.0)
CENTRE = 3.0 * (-205.0 / 72.0)
WEIGHTS = (8.0 / 5.0, -1.0 / 5.0, 8.0 / 315.0, -1.0 / 560.0)

SMEM = pl.BlockSpec(memory_space=pltpu.SMEM)
VMEM = pl.BlockSpec(memory_space=pltpu.VMEM)
PARAMS = pltpu.CompilerParams(vmem_limit_bytes=44 << 20)


def band(size):
    offset = np.abs(np.arange(size)[:, None] - np.arange(size)[None, :])
    matrix = np.zeros((size, size), np.float32)
    for reach, weight in enumerate(WHOLE, start=1):
        matrix[offset == reach] = weight
    return jnp.asarray(matrix, jnp.bfloat16)


def laplace(ref, x, band_ref):
    centre = ref[x + REACH]
    high = centre.astype(jnp.bfloat16)
    low = (centre - high.astype(jnp.float32)).astype(jnp.bfloat16)
    weights = band_ref[...]
    along_y = jnp.dot(
        jnp.concatenate([high, low], axis=1),
        jnp.concatenate([weights, weights], axis=0),
        preferred_element_type=jnp.float32,
    )
    along_z = jnp.dot(
        jnp.concatenate([weights, weights], axis=1),
        jnp.concatenate([high, low], axis=0),
        preferred_element_type=jnp.float32,
    )
    total = CENTRE * centre + (along_y + along_z) * (1.0 / UNIT)
    for reach, weight in enumerate(WEIGHTS, start=1):
        total = total + weight * (ref[x + REACH - reach] + ref[x + REACH + reach])
    return total


def cut_kernel(shots, width_x, me_ref, ax_ref, ay_ref, model_ref, out_ref, near_ref, far_ref):
    width_y = out_ref.shape[1]
    first = me_ref[0] * width_x
    near_ref[...] = model_ref[:, :width_y]
    far_ref[...] = model_ref[:, width_y:]
    lane = lax.broadcasted_iota(jnp.int32, (width_x, width_y), 1)

    def body(shot, carry):
        rows = pl.ds(ax_ref[shot] + first, width_x)
        column = ay_ref[shot]
        turn = lax.rem(2 * width_y - column, width_y)
        near = pltpu.roll(near_ref[rows, :], turn, 1)
        far = pltpu.roll(far_ref[rows, :], turn, 1)
        start = pl.multiple_of(shot * width_x, width_x)
        out_ref[pl.ds(start, width_x), :] = jnp.where(lane < width_y - column, near, far)
        return carry

    lax.fori_loop(0, shots, body, 0, unroll=8)


def spread_kernel(shots, width_x, me_ref, ax_ref, ay_ref, in_ref, out_ref, near_ref, far_ref):
    width_y = in_ref.shape[1]
    first = me_ref[0] * width_x
    near_ref[...] = jnp.zeros_like(near_ref)
    far_ref[...] = jnp.zeros_like(far_ref)
    lane = lax.broadcasted_iota(jnp.int32, (width_x, width_y), 1)

    def body(shot, carry):
        start = pl.multiple_of(shot * width_x, width_x)
        column = ay_ref[shot]
        moved = pltpu.roll(in_ref[pl.ds(start, width_x), :], lax.rem(column, width_y), 1)
        rows = pl.ds(ax_ref[shot] + first, width_x)
        near_ref[rows, :] = near_ref[rows, :] + jnp.where(lane < column, 0.0, moved)
        far_ref[rows, :] = far_ref[rows, :] + jnp.where(lane < column, moved, 0.0)
        return carry

    lax.fori_loop(0, shots, body, 0, unroll=8)
    out_ref[:, :width_y] = near_ref[...]
    out_ref[:, width_y:] = far_ref[...]


def receiver_kernel(count, across, depth, index_ref, seen_ref, out_ref):
    width_y = out_ref.shape[2]
    out_ref[...] = jnp.zeros_like(out_ref)
    shape = out_ref.shape[1:]
    lane = lax.broadcasted_iota(jnp.int32, shape, 1)
    line = lax.broadcasted_iota(jnp.int32, shape, 0)

    def body(receiver, carry):
        flat = index_ref[receiver]
        cell_z = flat // (across * width_y)
        cell_x = flat // width_y % across
        cell_y = flat % width_y
        value = jnp.where(line == 1, seen_ref[0, receiver], 1.0)
        value = jnp.where(line == 2, seen_ref[1, receiver], value)
        value = jnp.where(line == 3, seen_ref[2, receiver], value)
        row = cell_x * depth + cell_z
        out_ref[row] = out_ref[row] + jnp.where(lane == cell_y, value, 0.0)
        return carry

    lax.fori_loop(0, count, body, 0, unroll=4)


def slab_slice(ref, first, depth, width_x, row):
    return ref[pl.ds(first + row, depth, stride=width_x), :]


def before_kernel(
    slabs, depth, width_x, me_ref, own_ref, left_ref, right_ref, far_a_ref, far_b_ref, band_ref,
    start_ref, push_ref, later_ref, back_ref, curve_ref, pad_ref,
):
    me = me_ref[0]
    block = depth * width_x
    outs = (start_ref, push_ref, later_ref, back_ref)
    for distance, pieces in (
        (0, [(own_ref, k) for k in range(4)]),
        (slabs - 1, [(left_ref, k) for k in range(4)]),
        (1, [(right_ref, k) for k in range(4)]),
        (2, [(far_a_ref, 0), (far_a_ref, 1), (far_b_ref, 0), (far_b_ref, 1)]),
    ):
        base = lax.rem(me + distance, slabs) * width_x
        for (ref, place), out in zip(pieces, outs):
            for row in range(width_x):
                out[base + row] = slab_slice(ref, place * block, depth, width_x, row)
    across = slabs * width_x
    zeros = jnp.zeros(pad_ref.shape[1:], jnp.float32)
    for row in range(REACH):
        pad_ref[row] = zeros
        pad_ref[REACH + across + row] = zeros

    def copy(x, carry):
        pad_ref[x + REACH] = start_ref[x]
        return carry

    lax.fori_loop(0, across, copy, 0)

    def curve(x, carry):
        curve_ref[x] = laplace(pad_ref, x, band_ref)
        return carry

    lax.fori_loop(0, across, curve, 0)


def main_kernel(
    slabs, depth, width_x, me_ref, source_ref, wave_ref, own_ref, left_ref, right_ref, far_ref,
    start_ref, push_ref, later_ref, back_ref, curve_ref, extra_ref, band_ref,
    grad_ref, first_ref, second_ref,
    speed_ref, one_ref, two_ref, scaled_ref, again_ref, curve_one_ref, lam_ref, lam_two_ref, sum_ref, mark_ref,
):
    me = me_ref[0]
    across = slabs * width_x
    width_y = mark_ref.shape[1]
    for distance, ref in ((0, own_ref), (slabs - 1, left_ref), (1, right_ref), (2, far_ref)):
        base = lax.rem(me + distance, slabs) * width_x
        for row in range(width_x):
            speed_ref[base + row] = slab_slice(ref, 0, depth, width_x, row)
    zeros = jnp.zeros((depth, width_y), jnp.float32)
    for ref in (one_ref, two_ref, scaled_ref, again_ref):
        for row in range(REACH):
            ref[row] = zeros
            ref[REACH + across + row] = zeros
    flat = source_ref[0]
    source_z = flat // (across * width_y)
    source_x = flat // width_y % across
    source_y = flat % width_y
    spot_z = lax.broadcasted_iota(jnp.int32, (depth, width_y), 0) == source_z
    spot_y = lax.broadcasted_iota(jnp.int32, (depth, width_y), 1) == source_y
    mark_ref[...] = jnp.where(spot_z & spot_y, 1.0, 0.0)

    def pulse(x, step):
        return mark_ref[...] * jnp.where(x == source_x, wave_ref[0, step], 0.0)

    def extra(x, line):
        return extra_ref[pl.ds(x * (depth * 4) + line, depth, stride=4), :]

    def step_one(x, carry):
        speed = speed_ref[x]
        one_ref[x + REACH] = push_ref[x] + speed * curve_ref[x] + pulse(x, 0)
        scaled_ref[x + REACH] = speed * later_ref[x]
        return carry

    lax.fori_loop(0, across, step_one, 0)

    def step_two(x, carry):
        bend = laplace(one_ref, x, band_ref)
        curve_one_ref[x] = bend
        two_ref[x + REACH] = 2.0 * one_ref[x + REACH] - start_ref[x] + speed_ref[x] * bend + pulse(x, 1)
        return carry

    lax.fori_loop(0, across, step_two, 0)

    def reach(slices):
        low = jnp.maximum(me * width_x - slices, 0)
        return low, jnp.minimum((me + 1) * width_x + slices, across)

    def back_three(x, carry):
        speed = speed_ref[x]
        bend = laplace(two_ref, x, band_ref)
        three = 2.0 * two_ref[x + REACH] - one_ref[x + REACH] + speed * bend + pulse(x, 2)
        lam = back_ref[x] + laplace(scaled_ref, x, band_ref)
        lam = lam + (extra(x, 0) * three - extra(x, 3))
        lam_ref[x] = lam
        sum_ref[x] = lam * bend
        again_ref[x + REACH] = speed * lam
        return carry

    low, high = reach(2 * REACH)
    lax.fori_loop(low, high, back_three, 0)

    def back_two(x, carry):
        lam = 2.0 * lam_ref[x] - later_ref[x] + laplace(again_ref, x, band_ref)
        lam = lam + (extra(x, 0) * two_ref[x + REACH] - extra(x, 2))
        lam_two_ref[x] = lam
        sum_ref[x] = sum_ref[x] + lam * curve_one_ref[x]
        scaled_ref[x + REACH] = speed_ref[x] * lam
        return carry

    low, high = reach(REACH)
    lax.fori_loop(low, high, back_two, 0)

    for row in range(width_x):
        x = me * width_x + row
        lam = 2.0 * lam_two_ref[x] - lam_ref[x] + laplace(scaled_ref, x, band_ref)
        lam = lam + (extra(x, 0) * one_ref[x + REACH] - extra(x, 1))
        first_ref[row] = lam.astype(first_ref.dtype)
        second_ref[row] = lam_two_ref[x].astype(second_ref.dtype)
        grad_ref[pl.ds(row, depth, stride=width_x), :] = sum_ref[x] + lam * curve_ref[x]


def shift(x, distance):
    count = lax.axis_size("sub")
    return lax.ppermute(x, "sub", [(i, (i + distance) % count) for i in range(count)])


def per_device(
    model,
    anchor_x,
    anchor_y,
    state_before,
    state_now,
    adjoint_later,
    adjoint_latest,
    wavelet,
    src_index,
    rec_index,
    observed,
):
    groups = lax.axis_size("shots")
    slabs = lax.axis_size("sub")
    _, model_x, model_y = model.shape
    depth, width_x, width_y = state_now.shape[1:]
    across = width_x * slabs
    block = depth * width_x
    me = lax.axis_index("sub").astype(jnp.int32)[None]
    weights = band(width_y)
    f32 = jnp.float32

    def shape(*dims):
        return jax.ShapeDtypeStruct(dims, f32)

    now = state_now[0].astype(f32)
    later = adjoint_later[0].astype(f32)
    fields = jnp.stack(
        [
            now,
            2.0 * now - state_before[0].astype(f32),
            later,
            2.0 * later - adjoint_latest[0].astype(f32),
        ]
    ).reshape(4 * block, width_y)
    left = shift(fields, 1)
    right = shift(fields, -1)
    far_a = shift(left[: 2 * block], 1)
    far_b = shift(right[2 * block :], -1)

    panels = pl.pallas_call(
        functools.partial(cut_kernel, groups, width_x),
        out_shape=shape(groups * width_x, width_y),
        in_specs=[SMEM, SMEM, SMEM, VMEM],
        out_specs=VMEM,
        scratch_shapes=[pltpu.VMEM((model_x, width_y), f32)] * 2,
        compiler_params=PARAMS,
        name="cut",
    )(me, anchor_x, anchor_y, model[0])
    speed = lax.all_to_all(
        panels.reshape(groups, width_x, width_y), "shots", split_axis=0, concat_axis=0, tiled=True
    ).reshape(block, width_y)

    extra = pl.pallas_call(
        functools.partial(receiver_kernel, rec_index.shape[1], across, depth),
        out_shape=shape(across * depth, 4, width_y),
        in_specs=[SMEM, SMEM],
        out_specs=VMEM,
        compiler_params=PARAMS,
        name="receivers",
    )(rec_index[0], observed[0]).reshape(across * depth * 4, width_y)

    whole = (across, depth, width_y)
    padded = (across + 2 * REACH, depth, width_y)
    start, push, late, back, curve = pl.pallas_call(
        functools.partial(before_kernel, slabs, depth, width_x),
        out_shape=[shape(*whole)] * 5,
        in_specs=[SMEM] + [VMEM] * 6,
        out_specs=[VMEM] * 5,
        scratch_shapes=[pltpu.VMEM(padded, f32)],
        compiler_params=PARAMS,
        name="before",
    )(me, fields, left, right, far_a, far_b, weights)

    speed_left = shift(speed, 1)
    speed_right = shift(speed, -1)
    speed_far = shift(speed, 2)

    slab = jax.ShapeDtypeStruct((width_x, depth, width_y), jnp.bfloat16)
    grad, first, second = pl.pallas_call(
        functools.partial(main_kernel, slabs, depth, width_x),
        out_shape=[shape(block, width_y), slab, slab],
        in_specs=[SMEM] * 3 + [VMEM] * 11,
        out_specs=[VMEM] * 3,
        scratch_shapes=[
            pltpu.VMEM(whole, f32),
            pltpu.VMEM(padded, f32),
            pltpu.VMEM(padded, f32),
            pltpu.VMEM(padded, f32),
            pltpu.VMEM(padded, f32),
            pltpu.VMEM(whole, f32),
            pltpu.VMEM(whole, f32),
            pltpu.VMEM(whole, f32),
            pltpu.VMEM(whole, f32),
            pltpu.VMEM((depth, width_y), f32),
        ],
        compiler_params=PARAMS,
        name="window",
    )(
        me, src_index, wavelet, speed, speed_left, speed_right, speed_far,
        start, push, late, back, curve, extra, weights,
    )

    returned = lax.all_to_all(
        grad.reshape(groups, width_x, width_y), "shots", split_axis=0, concat_axis=0, tiled=True
    ).reshape(groups * width_x, width_y)
    owned = pl.pallas_call(
        functools.partial(spread_kernel, groups, width_x),
        out_shape=shape(model_x, model_y),
        in_specs=[SMEM, SMEM, SMEM, VMEM],
        out_specs=VMEM,
        scratch_shapes=[pltpu.VMEM((model_x, width_y), f32)] * 2,
        compiler_params=PARAMS,
        name="spread",
    )(me, anchor_x, anchor_y, returned)
    parts = lax.all_to_all(
        owned.reshape(slabs, model_x // slabs, model_y), "sub", split_axis=0, concat_axis=0, tiled=True
    )
    gradient = parts[0]
    for index in range(1, slabs):
        gradient = gradient + parts[index]
    return (
        gradient[None],
        jnp.transpose(first, (1, 0, 2))[None],
        jnp.transpose(second, (1, 0, 2))[None],
    )


def solution(mesh):
    return jax.shard_map(
        per_device,
        mesh=mesh,
        in_specs=(
            P("shots", None, None),
            P(),
            P(),
            P("shots", None, "sub", None),
            P("shots", None, "sub", None),
            P("shots", None, "sub", None),
            P("shots", None, "sub", None),
            P("shots", None),
            P("shots"),
            P("shots", None),
            P("shots", None, None),
        ),
        out_specs=(
            P("shots", "sub", None),
            P("shots", None, "sub", None),
            P("shots", None, "sub", None),
        ),
        check_vma=False,
    )
```

time: 1180 us -> 143 us (0.12); the launches traced: 1160 us -> 141 us
  other arithmetic: 569 us -> 4.08 us
  local copies, waits for them, and re-layouts: 438 us -> 8.24 us
  waiting for transfers between devices: 77.5 us -> 21.4 us
  Pallas kernels: 0 us -> 29.7 us
  blocking collectives: 0 us -> 28.6 us
  between operations: 22.6 us -> 1.54 us
    scatter-add x4 -> x0, other arithmetic: 541 us -> none  [the longest x1 452 us: per_device(): owned = owned.at[:, flat_cells].add(jnp.moveaxis(returned, 1, 0))]
    gather x387 -> x0, local copies, waits for them, and re-layouts: 430 us -> none
    ppermute x12 -> x7, waiting for transfers between devices: 31.8 us -> 0.02 us  [shift(): lax.ppermute(x, 'sub', [(i, (i + distance) % count) for i in range(count)])]
    pallas_call x0 -> x5, Pallas kernels: none -> 29.7 us  [the longest x1 10.9 us: per_device(): pl.pallas_call(functools.partial(main_kernel, slabs, depth, width_x), out...]
    all_to_all x0 -> x1, blocking collectives: none -> 28.6 us  [per_device(): lax.all_to_all(grad.reshape(groups, width_x, width_y), 'shots', split_axi...]
    reduce_scatter x1 -> x0, waiting for transfers between devices: 17.2 us -> none  [per_device(): gradient = lax.psum_scatter(owned, 'sub', scatter_dimension=1, tiled=True)]
    ppermute x12 -> x7, starting transfers between devices: 28 us -> 23.6 us  [shift(): lax.ppermute(x, 'sub', [(i, (i + distance) % count) for i in range(count)])]
  transfers between devices with their start and end apart: 15 -> 9, of which waited for: 10 -> 2; matrix products, arithmetic and copies ran while one was open for 2% -> 2% of each run, Pallas kernels for 0% -> 11%
where the time goes in v1:
time: 143 us; the launch traced here: 141 us
  starting transfers between devices  47.9 us (33%)
  Pallas kernels  29.7 us (21%)
  blocking collectives  28.6 us (20%)
  waiting for transfers between devices  21.4 us (15%)
  local copies, waits for them, and re-layouts  8.24 us (6%)
  other arithmetic  4.08 us (3%)
  between operations  1.54 us (1%)
    all_to_all x1, blocking collectives, per_device(): lax.all_to_all(grad.reshape(groups, width_x, width_y), 'shots', split_axi...  28.6 us
    ppermute x7, starting transfers between devices, shift(): lax.ppermute(x, 'sub', [(i, (i + distance) % count) for i in range(count)])  23.6 us
    all_to_all x1, starting transfers between devices, per_device(): lax.all_to_all(panels.reshape(groups, width_x, width_y), 'shots', split_a...  19.3 us
    all_to_all x1, waiting for transfers between devices, per_device(): lax.all_to_all(panels.reshape(groups, width_x, width_y), 'shots', split_a...  13.1 us
    pallas_call x1, Pallas kernels, per_device(): pl.pallas_call(functools.partial(main_kernel, slabs, depth, width_x), out...  10.9 us
    pallas_call x1, Pallas kernels, per_device(): pl.pallas_call(functools.partial(receiver_kernel, rec_index.shape[1], acr...  9.12 us
    all_to_all x1, waiting for transfers between devices, per_device(): lax.all_to_all(owned.reshape(slabs, model_x // slabs, model_y), 'sub', sp...  8.24 us
    unnamed x25, local copies, waits for them, and re-layouts  6.55 us
  transfers between devices with their start and end apart: 9, of which 2 were waited for; matrix products, arithmetic and copies ran while one was open for 2% of the time, Pallas kernels for 11%

profile of v1, /device:TPU:24, one launch (start us, length us, event | category | flops | bytes accessed | tf_op | source)
XLA Modules:
  0.0 141.4 jit_solution(7505581997754122155)
XLA Ops:
  0.6 0.0 copy-start.10
  0.6 0.0 copy-start.4
  0.7 0.9 convert_element_type.18
  1.6 0.9 convert_element_type.20
  2.5 1.3 convert_subtract_fusion
  3.8 0.0 copy-start.3
  3.8 0.2 pad_maximum_fusion
  4.1 4.7 %collective-permute-start.4 = (f32[2048,128]{1,0:T(8,128)S(1)}, f32[2048,128]{1,0:T(8,128)S(1)}, u32[]{:S(2)}, u32[]{:S(2)}) collective-permute-start(f32[2048,128]{1,0:T(8,128)S(1)} %bitcast.20), channel_id=1, source_target_pairs={{0,3},{1,0},{2,1},{3,2},{4,7},{5,4},{6,5},{7,6},{8,11},{9,8},{10,9... | collective-permute-start | bytes 3145736 | tf_op jit(solution)/shard_map/ppermute | solution.py:243
  8.7 1.9 %collective-permute-start.3 = (f32[2048,128]{1,0:T(8,128)S(1)}, f32[2048,128]{1,0:T(8,128)S(1)}, u32[]{:S(2)}, u32[]{:S(2)}) collective-permute-start(f32[2048,128]{1,0:T(8,128)S(1)} %bitcast.21), channel_id=1, source_target_pairs={{0,1},{1,2},{2,3},{3,0},{4,5},{5,6},{6,7},{7,4},{8,9},{9,10},{10,1... | collective-permute-start | bytes 3145736 | tf_op jit(solution)/shard_map/ppermute | solution.py:243
  10.7 0.0 copy-start.2
  10.7 1.0 copy-done.2
  11.7 0.0 copy-start.5
  11.7 0.7 copy-done.5
  12.4 0.0 copy-start.7
  12.4 0.7 copy-done.7
  13.0 2.0 %cut.1 = f32[512,128]{1,0:T(8,128)S(1)} custom-call(s32[1]{0:T(128)} %bitcast.me_ref, s32[128]{0:T(128)S(1)} %copy-done.5, s32[128]{0:T(128)S(1)} %copy-done.7, f32[512,256]{1,0:T(8,128)S(1)} %bitcast.29), custom_call_target="tpu_custom_call" | custom-call | tf_op jit(solution)/shard_map/cut/pallas_call | solution.py:287
  15.1 0.0 copy-start.1
  15.1 0.7 copy-done.1
  15.8 19.3 %all-to-all-start = ((f32[128,4,128]{2,1,0:T(4,128)}), f32[128,4,128]{2,1,0:T(4,128)S(1)}, u32[]{:S(2)}, u32[]{:S(2)}) async-start(f32[128,4,128]{2,1,0:T(4,128)} %bitcast.27), calls=%async_computation | async-start | bytes 524288 | tf_op jit(solution)/shard_map/all_to_all | solution.py:296
  35.1 0.0 collective-permute-done.4.right_ref
  35.1 0.8 slice.25
  35.9 5.1 %collective-permute-start.6 = (f32[1024,128]{1,0:T(8,128)}, f32[1024,128]{1,0:T(8,128)}, u32[]{:S(2)}, u32[]{:S(2)}) collective-permute-start(f32[1024,128]{1,0:T(8,128)} %slice.25), channel_id=1, source_target_pairs={{0,3},{1,0},{2,1},{3,2},{4,7},{5,4},{6,5},{7,6},{8,11},{9,8},{10,9... | collective-permute-start | bytes 1572872 | tf_op jit(solution)/shard_map/ppermute | solution.py:243
  41.0 0.0 collective-permute-done.3.left_ref
  41.1 0.9 slice.24
  41.9 1.9 %collective-permute-start.5 = (f32[1024,128]{1,0:T(8,128)}, f32[1024,128]{1,0:T(8,128)}, u32[]{:S(2)}, u32[]{:S(2)}) collective-permute-start(f32[1024,128]{1,0:T(8,128)} %slice.24), channel_id=1, source_target_pairs={{0,1},{1,2},{2,3},{3,0},{4,5},{5,6},{6,7},{7,4},{8,9},{9,10},{10,1... | collective-permute-start | bytes 1572872 | tf_op jit(solution)/shard_map/ppermute | solution.py:243
  43.8 13.1 %all-to-all-done = f32[128,4,128]{2,1,0:T(4,128)S(1)} async-done(((f32[128,4,128]{2,1,0:T(4,128)}), f32[128,4,128]{2,1,0:T(4,128)S(1)}, u32[]{:S(2)}, u32[]{:S(2)}) %all-to-all-start) | async-done | bytes 262176 | tf_op jit(solution)/shard_map/all_to_all | solution.py:296
  57.0 4.2 %collective-permute-start.2 = (f32[512,128]{1,0:T(8,128)S(1)}, f32[512,128]{1,0:T(8,128)S(1)}, u32[]{:S(2)}, u32[]{:S(2)}) collective-permute-start(f32[512,128]{1,0:T(8,128)S(1)} %bitcast.23), channel_id=1, source_target_pairs={{0,2},{1,3},{2,0},{3,1},{4,6},{5,7},{6,4},{7,5},{8,10},{9,11},{10,... | collective-permute-start | bytes 786440 | tf_op jit(solution)/shard_map/ppermute | solution.py:243
  61.2 3.0 %collective-permute-start.1 = (f32[512,128]{1,0:T(8,128)S(1)}, f32[512,128]{1,0:T(8,128)S(1)}, u32[]{:S(2)}, u32[]{:S(2)}) collective-permute-start(f32[512,128]{1,0:T(8,128)S(1)} %bitcast.24), channel_id=1, source_target_pairs={{0,3},{1,0},{2,1},{3,2},{4,7},{5,4},{6,5},{7,6},{8,11},{9,8},{10,9... | collective-permute-start | bytes 786440 | tf_op jit(solution)/shard_map/ppermute | solution.py:243
  64.2 2.8 %collective-permute-start = (f32[512,128]{1,0:T(8,128)S(1)}, f32[512,128]{1,0:T(8,128)S(1)}, u32[]{:S(2)}, u32[]{:S(2)}) collective-permute-start(f32[512,128]{1,0:T(8,128)S(1)} %bitcast.25), channel_id=1, source_target_pairs={{0,1},{1,2},{2,3},{3,0},{4,5},{5,6},{6,7},{7,4},{8,9},{9,10},{10,1... | collective-permute-start | bytes 786440 | tf_op jit(solution)/shard_map/ppermute | solution.py:243
  67.7 0.0 copy-done.10
  67.7 0.0 copy-done.4
  67.7 0.0 copy-start.9
  67.7 9.1 %receivers.1 = f32[2048,4,128]{2,1,0:T(4,128)S(1)} custom-call(s32[512]{0:T(512)S(1)} %bitcast.34, f32[3,512]{1,0:T(4,128)S(1)} %bitcast.33), custom_call_target="tpu_custom_call" | custom-call | tf_op jit(solution)/shard_map/receivers/pallas_call | solution.py:300
  76.8 0.0 copy-start
  76.8 1.9 %copy-done = f32[2048,4,128]{2,1,0:T(4,128)} copy-done((f32[2048,4,128]{2,1,0:T(4,128)}, f32[2048,4,128]{2,1,0:T(4,128)S(1)}, u32[]{:S(2)}) %copy-start) | copy-done | bytes 4194328
  78.8 0.0 collective-permute-done.6.far_b_ref
  78.8 0.0 collective-permute-done.5.far_a_ref
  78.8 0.0 copy-done.3
  78.8 4.6 %before.1 = (f32[16,128,128]{2,1,0:T(8,128)S(1)}, f32[16,128,128]{2,1,0:T(8,128)S(1)}, f32[16,128,128]{2,1,0:T(8,128)S(1)}, f32[16,128,128]{2,1,0:T(8,128)S(1)}, f32[16,128,128]{2,1,0:T(8,128)S(1)}) custom-call(s32[1]{0:T(128)} %bitcast.me_ref, f32[2048,128]{1,0:T(8,128)S(1)} %bitcast.22, f32[2048,128]{1,0:T(8,128)S(1)} %collective-permute-done.3.left_ref, ...), custom_call_target="tpu_custom_call" | custom-call | tf_op jit(solution)/shard_map/before/pallas_call | solution.py:311
  83.4 0.0 collective-permute-done.2.far_ref
  83.4 0.0 collective-permute-done.1.right_ref
  83.5 0.0 collective-permute-done.left_ref
  83.5 0.0 copy-done.9
  83.5 0.0 copy-start.6
  83.5 0.0 copy-start.8
  83.5 10.9 %window.1 = (f32[512,128]{1,0:T(8,128)S(1)}, bf16[4,128,128]{2,1,0:T(8,128)(2,1)S(1)}, bf16[4,128,128]{2,1,0:T(8,128)(2,1)S(1)}) custom-call(s32[1]{0:T(128)} %bitcast.me_ref, s32[1]{0:T(128)S(6)} %copy.20.source_ref, f32[1,3]{1,0:T(1,128)S(1)} %copy-done.9, f32[512,128]{1,0:T(8,128)S(1)} %bitcast.26, f32[512,128]{1,0:T(8,128)S(1)} %collective-permute-done.left_ref, ...), custom_call_target="tpu_custom_call" | custom-call | tf_op jit(solution)/shard_map/window/pallas_call | solution.py:326
  94.4 28.6 %all_to_all.15 = f32[128,4,128]{2,1,0:T(4,128)S(1)} all-to-all(f32[128,4,128]{2,1,0:T(4,128)S(1)} %bitcast.30), channel_id=1, replica_groups=mesh['shots'=128,'sub'=4] {'shots'}, dimensions={0} | all-to-all | bytes 524288 | tf_op jit(solution)/shard_map/all_to_all | solution.py:350
  123.0 0.0 copy-done.6
  123.0 0.0 copy-done.8
  123.0 3.0 %spread.1 = f32[512,256]{1,0:T(8,128)} custom-call(s32[1]{0:T(128)} %bitcast.me_ref, s32[128]{0:T(128)S(1)} %copy-done.6, s32[128]{0:T(128)S(1)} %copy-done.8, f32[512,128]{1,0:T(8,128)S(1)} %bitcast.28), custom_call_target="tpu_custom_call" | custom-call | tf_op jit(solution)/shard_map/spread/pallas_call | solution.py:353
  126.0 4.9 %all-to-all-start.2 = ((f32[4,128,256]{2,1,0:T(8,128)}), f32[4,128,256]{2,1,0:T(8,128)S(1)}, u32[]{:S(2)}, u32[]{:S(2)}) async-start(f32[4,128,256]{2,1,0:T(8,128)} %bitcast.9), calls=%async_computation.2 | async-start | bytes 1048576 | tf_op jit(solution)/shard_map/all_to_all | solution.py:362
  131.0 0.8 copy.15
  131.7 0.8 copy.16
  132.5 8.2 %all-to-all-done.2 = f32[4,128,256]{2,1,0:T(8,128)S(1)} async-done(((f32[4,128,256]{2,1,0:T(8,128)}), f32[4,128,256]{2,1,0:T(8,128)S(1)}, u32[]{:S(2)}, u32[]{:S(2)}) %all-to-all-start.2) | async-done | bytes 524320 | tf_op jit(solution)/shard_map/all_to_all | solution.py:362
  140.7 0.7 slice_add_fusion
  (1 shorter events, 0.0 us)
Async XLA Ops:
  0.6 67.0 %copy-start.10 = (f32[1,3,512]{2,0,1:T(1,128)S(1)}, f32[1,3,512]{2,0,1:T(1,128)}, u32[]{:S(2)}) copy-start(f32[1,3,512]{2,0,1:T(1,128)} %param.22) | copy-start | bytes 18436
  0.6 67.0 %copy-start.4 = (s32[1,512]{1,0:T(1,128)S(1)}, s32[1,512]{1,0:T(1,128)}, u32[]{:S(2)}) copy-start(s32[1,512]{1,0:T(1,128)} %param.21) | copy-start | bytes 6148
  3.8 75.0 %copy-start.3 = (bf16[128,128]{1,0:T(8,128)(2,1)S(1)}, bf16[128,128]{1,0:T(8,128)(2,1)}, u32[]{:S(2)}) copy-start(bf16[128,128]{1,0:T(8,128)(2,1)} %constant.8.clone.band_ref) | copy-start | bytes 98308
  4.1 31.0 %collective-permute-start.4 = (f32[2048,128]{1,0:T(8,128)S(1)}, f32[2048,128]{1,0:T(8,128)S(1)}, u32[]{:S(2)}, u32[]{:S(2)}) collective-permute-start(f32[2048,128]{1,0:T(8,128)S(1)} %bitcast.20), channel_id=1, source_target_pairs={{0,3},{1,0},{2,1},{3,2},{4,7},{5,4},{6,5},{7,6},{8,11},{9,8},{10,9... | collective-permute-start | bytes 3145736 | tf_op jit(solution)/shard_map/ppermute | solution.py:243
  8.7 32.3 %collective-permute-start.3 = (f32[2048,128]{1,0:T(8,128)S(1)}, f32[2048,128]{1,0:T(8,128)S(1)}, u32[]{:S(2)}, u32[]{:S(2)}) collective-permute-start(f32[2048,128]{1,0:T(8,128)S(1)} %bitcast.21), channel_id=1, source_target_pairs={{0,1},{1,2},{2,3},{3,0},{4,5},{5,6},{6,7},{7,4},{8,9},{9,10},{10,1... | collective-permute-start | bytes 3145736 | tf_op jit(solution)/shard_map/ppermute | solution.py:243
  10.7 1.0 copy-start.2
  11.7 0.7 copy-start.5
  12.4 0.7 copy-start.7
  15.1 0.7 copy-start.1
  15.8 41.2 %all-to-all-start = ((f32[128,4,128]{2,1,0:T(4,128)}), f32[128,4,128]{2,1,0:T(4,128)S(1)}, u32[]{:S(2)}, u32[]{:S(2)}) async-start(f32[128,4,128]{2,1,0:T(4,128)} %bitcast.27), calls=%async_computation | async-start | bytes 524288 | tf_op jit(solution)/shard_map/all_to_all | solution.py:296
  35.9 42.9 %collective-permute-start.6 = (f32[1024,128]{1,0:T(8,128)}, f32[1024,128]{1,0:T(8,128)}, u32[]{:S(2)}, u32[]{:S(2)}) collective-permute-start(f32[1024,128]{1,0:T(8,128)} %slice.25), channel_id=1, source_target_pairs={{0,3},{1,0},{2,1},{3,2},{4,7},{5,4},{6,5},{7,6},{8,11},{9,8},{10,9... | collective-permute-start | bytes 1572872 | tf_op jit(solution)/shard_map/ppermute | solution.py:243
  41.9 36.9 %collective-permute-start.5 = (f32[1024,128]{1,0:T(8,128)}, f32[1024,128]{1,0:T(8,128)}, u32[]{:S(2)}, u32[]{:S(2)}) collective-permute-start(f32[1024,128]{1,0:T(8,128)} %slice.24), channel_id=1, source_target_pairs={{0,1},{1,2},{2,3},{3,0},{4,5},{5,6},{6,7},{7,4},{8,9},{9,10},{10,1... | collective-permute-start | bytes 1572872 | tf_op jit(solution)/shard_map/ppermute | solution.py:243
  57.0 26.5 %collective-permute-start.2 = (f32[512,128]{1,0:T(8,128)S(1)}, f32[512,128]{1,0:T(8,128)S(1)}, u32[]{:S(2)}, u32[]{:S(2)}) collective-permute-start(f32[512,128]{1,0:T(8,128)S(1)} %bitcast.23), channel_id=1, source_target_pairs={{0,2},{1,3},{2,0},{3,1},{4,6},{5,7},{6,4},{7,5},{8,10},{9,11},{10,... | collective-permute-start | bytes 786440 | tf_op jit(solution)/shard_map/ppermute | solution.py:243
  61.2 22.3 %collective-permute-start.1 = (f32[512,128]{1,0:T(8,128)S(1)}, f32[512,128]{1,0:T(8,128)S(1)}, u32[]{:S(2)}, u32[]{:S(2)}) collective-permute-start(f32[512,128]{1,0:T(8,128)S(1)} %bitcast.24), channel_id=1, source_target_pairs={{0,3},{1,0},{2,1},{3,2},{4,7},{5,4},{6,5},{7,6},{8,11},{9,8},{10,9... | collective-permute-start | bytes 786440 | tf_op jit(solution)/shard_map/ppermute | solution.py:243
  64.2 19.2 %collective-permute-start = (f32[512,128]{1,0:T(8,128)S(1)}, f32[512,128]{1,0:T(8,128)S(1)}, u32[]{:S(2)}, u32[]{:S(2)}) collective-permute-start(f32[512,128]{1,0:T(8,128)S(1)} %bitcast.25), channel_id=1, source_target_pairs={{0,1},{1,2},{2,3},{3,0},{4,5},{5,6},{6,7},{7,4},{8,9},{9,10},{10,1... | collective-permute-start | bytes 786440 | tf_op jit(solution)/shard_map/ppermute | solution.py:243
  67.7 15.8 %copy-start.9 = (f32[1,3]{1,0:T(1,128)S(1)}, f32[1,3]{1,0:T(1,128)}, u32[]{:S(2)}) copy-start(f32[1,3]{1,0:T(1,128)} %wave_ref.1) | copy-start | bytes 40
  76.8 1.9 %copy-start = (f32[2048,4,128]{2,1,0:T(4,128)}, f32[2048,4,128]{2,1,0:T(4,128)S(1)}, u32[]{:S(2)}) copy-start(f32[2048,4,128]{2,1,0:T(4,128)S(1)} %receivers.1) | copy-start | bytes 12582916
  83.5 39.5 %copy-start.6 = (s32[128]{0:T(128)S(1)}, s32[128]{0:T(128)}, u32[]{:S(2)}) copy-start(s32[128]{0:T(128)} %ax_ref.3) | copy-start | bytes 1540
  83.5 39.5 %copy-start.8 = (s32[128]{0:T(128)S(1)}, s32[128]{0:T(128)}, u32[]{:S(2)}) copy-start(s32[128]{0:T(128)} %ay_ref.3) | copy-start | bytes 1540
  126.0 14.7 %all-to-all-start.2 = ((f32[4,128,256]{2,1,0:T(8,128)}), f32[4,128,256]{2,1,0:T(8,128)S(1)}, u32[]{:S(2)}, u32[]{:S(2)}) async-start(f32[4,128,256]{2,1,0:T(8,128)} %bitcast.9), calls=%async_computation.2 | async-start | bytes 1048576 | tf_op jit(solution)/shard_map/all_to_all | solution.py:362

commit v2 on v1

v2 whole, which is shorter than its diff:
```python
import functools

import jax
import jax.numpy as jnp
import numpy as np
from jax import lax
from jax.experimental import pallas as pl
from jax.experimental.pallas import tpu as pltpu
from jax.sharding import PartitionSpec as P

STEPS = 3
REACH = 4
UNIT = 5040.0
WHOLE = (8064.0, -1008.0, 128.0, -9.0)
CENTRE = 3.0 * (-205.0 / 72.0)
WEIGHTS = (8.0 / 5.0, -1.0 / 5.0, 8.0 / 315.0, -1.0 / 560.0)

SMEM = pl.BlockSpec(memory_space=pltpu.SMEM)
HBM = pl.BlockSpec(memory_space=pltpu.HBM)
VMEM = pl.BlockSpec(memory_space=pltpu.VMEM)
PARAMS = pltpu.CompilerParams(vmem_limit_bytes=24 << 20)


def band(size):
    offset = np.abs(np.arange(size)[:, None] - np.arange(size)[None, :])
    matrix = np.zeros((size, size), np.float32)
    for reach, weight in enumerate(WHOLE, start=1):
        matrix[offset == reach] = weight
    return jnp.asarray(matrix, jnp.bfloat16)


ROWS = 16


def along(ref, x, count, band_ref, part_ref):
    weights = band_ref[...]
    twice_down = jnp.concatenate([weights, weights], axis=0)
    twice_across = jnp.concatenate([weights, weights], axis=1)
    for index in range(count):
        centre = ref[x + REACH + index]
        high = centre.astype(jnp.bfloat16)
        low = (centre - high.astype(jnp.float32)).astype(jnp.bfloat16)
        along_y = jnp.dot(jnp.concatenate([high, low], axis=1), twice_down, preferred_element_type=jnp.float32)
        along_z = jnp.dot(twice_across, jnp.concatenate([high, low], axis=0), preferred_element_type=jnp.float32)
        part_ref[index] = along_y + along_z


def laplace(ref, x, count, rows, part_ref):
    near = [ref[x + index, rows, :] for index in range(count + 2 * REACH)]
    totals = []
    for index in range(count):
        centre = index + REACH
        total = CENTRE * near[centre] + part_ref[index, rows, :] * (1.0 / UNIT)
        for reach, weight in enumerate(WEIGHTS, start=1):
            total = total + weight * (near[centre - reach] + near[centre + reach])
        totals.append(total)
    return totals


def over_rows(depth, step):
    def body(index, carry):
        step(pl.ds(pl.multiple_of(index * ROWS, ROWS), ROWS), pl.multiple_of(index * ROWS, ROWS))
        return carry

    lax.fori_loop(0, depth // ROWS, body, 0, unroll=2)


def spread_kernel(shots, width_x, me_ref, ax_ref, ay_ref, in_ref, out_ref, near_ref, far_ref):
    width_y = in_ref.shape[1]
    first = me_ref[0] * width_x
    near_ref[...] = jnp.zeros_like(near_ref)
    far_ref[...] = jnp.zeros_like(far_ref)
    lane = lax.broadcasted_iota(jnp.int32, (width_x, width_y), 1)

    def body(shot, carry):
        start = pl.multiple_of(shot * width_x, width_x)
        column = ay_ref[shot]
        moved = pltpu.roll(in_ref[pl.ds(start, width_x), :], lax.rem(column, width_y), 1)
        rows = pl.ds(ax_ref[shot] + first, width_x)
        near_ref[rows, :] = near_ref[rows, :] + jnp.where(lane < column, 0.0, moved)
        far_ref[rows, :] = far_ref[rows, :] + jnp.where(lane < column, moved, 0.0)
        return carry

    lax.fori_loop(0, shots, body, 0, unroll=8)
    out_ref[:, :width_y] = near_ref[...]
    out_ref[:, width_y:] = far_ref[...]


def cell(flat, across, width_y):
    shift_y = width_y.bit_length() - 1
    shift_x = across.bit_length() - 1
    row = lax.shift_right_logical(flat, shift_y)
    return lax.shift_right_logical(row, shift_x), row & (across - 1), flat & (width_y - 1)


def receiver_kernel(count, across, depth, index_ref, seen_ref, out_ref):
    width_y = out_ref.shape[2]
    out_ref[...] = jnp.zeros_like(out_ref)
    shape = out_ref.shape[1:]
    lane = lax.broadcasted_iota(jnp.int32, shape, 1)
    line = lax.broadcasted_iota(jnp.int32, shape, 0)

    def body(receiver, carry):
        cell_z, cell_x, cell_y = cell(index_ref[receiver], across, width_y)
        value = jnp.where(line == 1, seen_ref[0, 0, receiver], 1.0)
        value = jnp.where(line == 2, seen_ref[1, 0, receiver], value)
        value = jnp.where(line == 3, seen_ref[2, 0, receiver], value)
        row = cell_x * depth + cell_z
        out_ref[row] = out_ref[row] + jnp.where(lane == cell_y, value, 0.0)
        return carry

    lax.fori_loop(0, count, body, 0, unroll=4)


def first_kernel(
    shots, depth, width_x, me_ref, ax_ref, ay_ref, model_hbm, before_hbm, now_hbm, later_hbm, latest_hbm,
    fields_hbm, panels_hbm,
    near_ref, far_ref, before_ref, now_ref, later_ref, latest_ref, turn_ref, fields_ref, panels_ref, in_sems, out_sems,
):
    block = depth * width_x
    width_y = panels_ref.shape[1]
    pairs = (
        (now_hbm, now_ref),
        (before_hbm, before_ref),
        (later_hbm, later_ref),
        (latest_hbm, latest_ref),
        (model_hbm.at[:, :width_y], near_ref),
        (model_hbm.at[:, width_y:], far_ref),
    )
    loads = [pltpu.make_async_copy(source, ref, in_sems.at[k]) for k, (source, ref) in enumerate(pairs)]
    for load in loads:
        load.start()

    def put(place, value):
        turn_ref[...] = value
        flat = turn_ref.reshape(block, width_y)
        for row in range(width_x):
            fields_ref[pl.ds(place * block + row * depth, depth), :] = flat[pl.ds(row, depth, stride=width_x), :]

    for load in loads[:4]:
        load.wait()
    now = now_ref[...].astype(jnp.float32)
    put(0, now)
    put(1, 2.0 * now - before_ref[...].astype(jnp.float32))
    later = later_ref[...].astype(jnp.float32)
    put(2, later)
    put(3, 2.0 * later - latest_ref[...].astype(jnp.float32))
    keep_fields = pltpu.make_async_copy(fields_ref, fields_hbm, out_sems.at[0])
    keep_fields.start()
    for load in loads[4:]:
        load.wait()
    first = me_ref[0] * width_x
    lane = lax.broadcasted_iota(jnp.int32, (width_x, width_y), 1)

    def cut(shot, carry):
        rows = pl.ds(ax_ref[shot] + first, width_x)
        column = ay_ref[shot]
        turn = lax.rem(2 * width_y - column, width_y)
        near = pltpu.roll(near_ref[rows, :], turn, 1)
        far = pltpu.roll(far_ref[rows, :], turn, 1)
        start = pl.multiple_of(shot * width_x, width_x)
        panels_ref[pl.ds(start, width_x), :] = jnp.where(lane < width_y - column, near, far)
        return carry

    lax.fori_loop(0, shots, cut, 0, unroll=8)
    keep_panels = pltpu.make_async_copy(panels_ref, panels_hbm, out_sems.at[1])
    keep_panels.start()
    keep_fields.wait()
    keep_panels.wait()


def slab_slice(ref, first, depth, width_x, row):
    return ref[pl.ds(first + row, depth, stride=width_x), :]


def before_kernel(
    slabs, depth, width_x, me_ref, own_ref, left_ref, right_ref, far_a_ref, far_b_ref, band_ref,
    start_ref, push_ref, later_ref, back_ref, curve_ref, part_ref, sems,
):
    me = me_ref[0]
    across = slabs * width_x
    outs = (start_ref, push_ref, later_ref, back_ref)
    copies = []
    for distance, pieces in (
        (0, [(own_ref, k) for k in range(4)]),
        (slabs - 1, [(left_ref, k) for k in range(4)]),
        (1, [(right_ref, k) for k in range(4)]),
        (2, [(far_a_ref, 0), (far_a_ref, 1), (far_b_ref, 0), (far_b_ref, 1)]),
    ):
        base = lax.rem(me + distance, slabs) * width_x
        for field, ((ref, place), out) in enumerate(zip(pieces, outs)):
            offset = REACH if field == 0 else 0
            source = ref.at[pl.ds(place * width_x, width_x)]
            target = out.at[pl.ds(base + offset, width_x)]
            copies.append((field, pltpu.make_async_copy(source, target, sems.at[field])))
    copies.sort(key=lambda item: item[0])
    for _, copy in copies:
        copy.start()
    zeros = jnp.zeros(start_ref.shape[1:], jnp.float32)
    for row in range(REACH):
        start_ref[row] = zeros
        start_ref[REACH + across + row] = zeros
    for field, copy in copies:
        if field == 0:
            copy.wait()

    def curve(slab, carry):
        x = slab * width_x
        along(start_ref, x, width_x, band_ref, part_ref)

        def step(rows, _):
            for index, bend in enumerate(laplace(start_ref, x, width_x, rows, part_ref)):
                curve_ref[x + index, rows, :] = bend

        over_rows(depth, step)
        return carry

    lax.fori_loop(0, slabs, curve, 0)
    for field, copy in copies:
        if field:
            copy.wait()


def main_kernel(
    slabs, depth, width_x, me_ref, source_ref, wave_ref, own_ref, left_ref, right_ref, far_ref,
    start_ref, push_ref, later_ref, back_ref, curve_ref, extra_ref, band_ref,
    grad_ref, first_ref, second_ref,
    speed_ref, one_ref, two_ref, scaled_ref, again_ref, curve_one_ref, lam_ref, lam_two_ref, sum_ref, mark_ref,
    part_ref, other_ref,
):
    me = me_ref[0]
    across = slabs * width_x
    width_y = mark_ref.shape[1]
    for distance, ref in ((0, own_ref), (slabs - 1, left_ref), (1, right_ref), (2, far_ref)):
        base = lax.rem(me + distance, slabs) * width_x
        for row in range(width_x):
            speed_ref[base + row] = slab_slice(ref, 0, depth, width_x, row)
    zeros = jnp.zeros((depth, width_y), jnp.float32)
    for ref in (one_ref, two_ref, scaled_ref, again_ref):
        for row in range(REACH):
            ref[row] = zeros
            ref[REACH + across + row] = zeros
    source_z, source_x, source_y = cell(source_ref[0], across, width_y)
    spot_z = lax.broadcasted_iota(jnp.int32, (depth, width_y), 0) == source_z
    spot_y = lax.broadcasted_iota(jnp.int32, (depth, width_y), 1) == source_y
    mark_ref[...] = jnp.where(spot_z & spot_y, 1.0, 0.0)

    def pulse(x, step, rows):
        return mark_ref[rows, :] * jnp.where(x == source_x, wave_ref[0, step], 0.0)

    def extra(x, line, first):
        return extra_ref[pl.ds((x * depth + first) * 4 + line, ROWS, stride=4), :]

    def by_slabs(step, slices):
        low = jnp.maximum(me - slices // width_x, 0)
        high = jnp.minimum(me + 1 + slices // width_x, slabs)

        def body(slab, carry):
            step(slab * width_x)
            return carry

        lax.fori_loop(low, high, body, 0)

    def step_one(x):
        def step(rows, _):
            for here in range(width_x):
                here = x + here
                speed = speed_ref[here, rows, :]
                one_ref[here + REACH, rows, :] = (
                    push_ref[here, rows, :] + speed * curve_ref[here, rows, :] + pulse(here, 0, rows)
                )
                scaled_ref[here + REACH, rows, :] = speed * later_ref[here, rows, :]

        over_rows(depth, step)

    by_slabs(step_one, across)

    def step_two(x):
        along(one_ref, x, width_x, band_ref, part_ref)

        def step(rows, _):
            for index, bend in enumerate(laplace(one_ref, x, width_x, rows, part_ref)):
                here = x + index
                curve_one_ref[here, rows, :] = bend
                two_ref[here + REACH, rows, :] = (
                    2.0 * one_ref[here + REACH, rows, :]
                    - start_ref[here + REACH, rows, :]
                    + speed_ref[here, rows, :] * bend
                    + pulse(here, 1, rows)
                )

        over_rows(depth, step)

    by_slabs(step_two, across)

    def back_three(x):
        along(two_ref, x, width_x, band_ref, part_ref)
        along(scaled_ref, x, width_x, band_ref, other_ref)

        def step(rows, first):
            bends = laplace(two_ref, x, width_x, rows, part_ref)
            backs = laplace(scaled_ref, x, width_x, rows, other_ref)
            for index, (bend, back) in enumerate(zip(bends, backs)):
                here = x + index
                speed = speed_ref[here, rows, :]
                three = (
                    2.0 * two_ref[here + REACH, rows, :]
                    - one_ref[here + REACH, rows, :]
                    + speed * bend
                    + pulse(here, 2, rows)
                )
                lam = back_ref[here, rows, :] + back
                lam = lam + (extra(here, 0, first) * three - extra(here, 3, first))
                lam_ref[here, rows, :] = lam
                sum_ref[here, rows, :] = lam * bend
                again_ref[here + REACH, rows, :] = speed * lam

        over_rows(depth, step)

    by_slabs(back_three, 2 * REACH)

    def back_two(x):
        along(again_ref, x, width_x, band_ref, part_ref)

        def step(rows, first):
            for index, back in enumerate(laplace(again_ref, x, width_x, rows, part_ref)):
                here = x + index
                lam = 2.0 * lam_ref[here, rows, :] - later_ref[here, rows, :] + back
                lam = lam + (extra(here, 0, first) * two_ref[here + REACH, rows, :] - extra(here, 2, first))
                lam_two_ref[here, rows, :] = lam
                sum_ref[here, rows, :] = sum_ref[here, rows, :] + lam * curve_one_ref[here, rows, :]
                scaled_ref[here + REACH, rows, :] = speed_ref[here, rows, :] * lam

        over_rows(depth, step)

    by_slabs(back_two, REACH)

    x = me * width_x
    along(scaled_ref, x, width_x, band_ref, part_ref)

    def step(rows, first):
        for index, back in enumerate(laplace(scaled_ref, x, width_x, rows, part_ref)):
            here = x + index
            lam_two = lam_two_ref[here, rows, :]
            lam = 2.0 * lam_two - lam_ref[here, rows, :] + back
            lam = lam + (extra(here, 0, first) * one_ref[here + REACH, rows, :] - extra(here, 1, first))
            first_ref[index, rows, :] = lam.astype(first_ref.dtype)
            second_ref[index, rows, :] = lam_two.astype(second_ref.dtype)
            grad_ref[pl.ds(first * width_x + index, ROWS, stride=width_x), :] = (
                sum_ref[here, rows, :] + lam * curve_ref[here, rows, :]
            )

    over_rows(depth, step)


def shift(x, distance):
    count = lax.axis_size("sub")
    return lax.ppermute(x, "sub", [(i, (i + distance) % count) for i in range(count)])


def per_device(
    model,
    anchor_x,
    anchor_y,
    state_before,
    state_now,
    adjoint_later,
    adjoint_latest,
    wavelet,
    src_index,
    rec_index,
    observed,
):
    groups = lax.axis_size("shots")
    slabs = lax.axis_size("sub")
    _, model_x, model_y = model.shape
    depth, width_x, width_y = state_now.shape[1:]
    across = width_x * slabs
    block = depth * width_x
    me = lax.axis_index("sub").astype(jnp.int32)[None]
    weights = band(width_y)
    f32 = jnp.float32

    def shape(*dims):
        return jax.ShapeDtypeStruct(dims, f32)

    state = pltpu.VMEM((depth, width_x, width_y), jnp.bfloat16)
    fields, panels = pl.pallas_call(
        functools.partial(first_kernel, groups, depth, width_x),
        out_shape=[shape(4 * block, width_y), shape(groups * width_x, width_y)],
        in_specs=[SMEM] * 3 + [HBM] * 5,
        out_specs=[HBM] * 2,
        scratch_shapes=[pltpu.VMEM((model_x, width_y), f32)] * 2
        + [state] * 4
        + [
            pltpu.VMEM((depth, width_x, width_y), f32),
            pltpu.VMEM((4 * block, width_y), f32),
            pltpu.VMEM((groups * width_x, width_y), f32),
            pltpu.SemaphoreType.DMA((6,)),
            pltpu.SemaphoreType.DMA((2,)),
        ],
        name="first",
    )(me, anchor_x, anchor_y, model[0], state_before[0], state_now[0], adjoint_later[0], adjoint_latest[0])
    left = shift(fields, 1)
    right = shift(fields, -1)
    far_a = shift(left[: 2 * block], 1)
    far_b = shift(right[2 * block :], -1)

    speed = lax.all_to_all(
        panels.reshape(groups, width_x, width_y), "shots", split_axis=0, concat_axis=0, tiled=True
    ).reshape(block, width_y)

    extra = pl.pallas_call(
        functools.partial(receiver_kernel, rec_index.shape[1], across, depth),
        out_shape=shape(across * depth, 4, width_y),
        in_specs=[SMEM, SMEM],
        out_specs=VMEM,
        compiler_params=PARAMS,
        name="receivers",
    )(rec_index[0], jnp.transpose(observed, (1, 0, 2))).reshape(across * depth * 4, width_y)

    whole = (across, depth, width_y)
    padded = (across + 2 * REACH, depth, width_y)
    start, push, late, back, curve = pl.pallas_call(
        functools.partial(before_kernel, slabs, depth, width_x),
        out_shape=[shape(*padded)] + [shape(*whole)] * 4,
        in_specs=[SMEM] + [HBM] * 5 + [VMEM],
        out_specs=[VMEM] * 5,
        scratch_shapes=[pltpu.VMEM((width_x, depth, width_y), f32), pltpu.SemaphoreType.DMA((4,))],
        compiler_params=PARAMS,
        name="before",
    )(me, *(piece.reshape(-1, depth, width_y) for piece in (fields, left, right, far_a, far_b)), weights)

    speed, extra = lax.optimization_barrier((speed, extra))
    speed_left = shift(speed, 1)
    speed_right = shift(speed, -1)
    speed_far = shift(speed, 2)

    slab = jax.ShapeDtypeStruct((width_x, depth, width_y), jnp.bfloat16)
    grad, first, second = pl.pallas_call(
        functools.partial(main_kernel, slabs, depth, width_x),
        out_shape=[shape(block, width_y), slab, slab],
        in_specs=[SMEM] * 3 + [VMEM] * 11,
        out_specs=[VMEM] * 3,
        scratch_shapes=[
            pltpu.VMEM(whole, f32),
            pltpu.VMEM(padded, f32),
            pltpu.VMEM(padded, f32),
            pltpu.VMEM(padded, f32),
            pltpu.VMEM(padded, f32),
            pltpu.VMEM(whole, f32),
            pltpu.VMEM(whole, f32),
            pltpu.VMEM(whole, f32),
            pltpu.VMEM(whole, f32),
            pltpu.VMEM((depth, width_y), f32),
            pltpu.VMEM((width_x, depth, width_y), f32),
            pltpu.VMEM((width_x, depth, width_y), f32),
        ],
        compiler_params=PARAMS,
        name="window",
    )(
        me, src_index, wavelet, speed, speed_left, speed_right, speed_far,
        start, push, late, back, curve, extra, weights,
    )

    returned = lax.all_to_all(
        grad.reshape(groups, width_x, width_y), "shots", split_axis=0, concat_axis=0, tiled=True
    ).reshape(groups * width_x, width_y)
    owned = pl.pallas_call(
        functools.partial(spread_kernel, groups, width_x),
        out_shape=shape(model_x, model_y),
        in_specs=[SMEM, SMEM, SMEM, VMEM],
        out_specs=VMEM,
        scratch_shapes=[pltpu.VMEM((model_x, width_y), f32)] * 2,
        compiler_params=PARAMS,
        name="spread",
    )(me, anchor_x, anchor_y, returned)
    parts = lax.all_to_all(
        owned.reshape(slabs, model_x // slabs, model_y), "sub", split_axis=0, concat_axis=0, tiled=True
    )
    gradient = parts[0]
    for index in range(1, slabs):
        gradient = gradient + parts[index]
    return (
        gradient[None],
        jnp.transpose(first, (1, 0, 2))[None],
        jnp.transpose(second, (1, 0, 2))[None],
    )


def solution(mesh):
    return jax.shard_map(
        per_device,
        mesh=mesh,
        in_specs=(
            P("shots", None, None),
            P(),
            P(),
            P("shots", None, "sub", None),
            P("shots", None, "sub", None),
            P("shots", None, "sub", None),
            P("shots", None, "sub", None),
            P("shots", None),
            P("shots"),
            P("shots", None),
            P("shots", None, None),
        ),
        out_specs=(
            P("shots", "sub", None),
            P("shots", None, "sub", None),
            P("shots", None, "sub", None),
        ),
        check_vma=False,
    )
```

time: 143 us -> 134 us (0.937)
  blocking collectives: 28.6 us -> 36.3 us
  Pallas kernels: 29.7 us -> 22.1 us
  waiting for transfers between devices: 21.4 us -> 17.8 us
  other arithmetic: 4.08 us -> 0.69 us
  local copies, waits for them, and re-layouts: 8.24 us -> 6.5 us
    all_to_all x1, waiting for transfers between devices: 13.1 us -> 3.51 us  [per_device(): lax.all_to_all(panels.reshape(groups, width_x, width_y), 'shots', split_a...]
    all_to_all x1, blocking collectives: 28.6 us -> 36.3 us  [per_device(): lax.all_to_all(grad.reshape(groups, width_x, width_y), 'shots', split_axi...]
    ppermute x7, waiting for transfers between devices: 0.02 us -> 6.03 us  [shift(): lax.ppermute(x, 'sub', [(i, (i + distance) % count) for i in range(count)])]
    pallas_call x1, Pallas kernels: 9.12 us -> 4.5 us  [per_device(): pl.pallas_call(functools.partial(receiver_kernel, rec_index.shape[1], acr...]
    pallas_call x1, Pallas kernels: 10.9 us -> 7.33 us  [per_device(): pl.pallas_call(functools.partial(main_kernel, slabs, depth, width_x), out...]
    pallas_call x1, Pallas kernels: 2.02 us -> 4.32 us  [per_device(): pl.pallas_call(functools.partial(first_kernel, groups, depth, width_x), o...]
    convert_element_type x2 -> x0, other arithmetic: 1.88 us -> none  [the longest x1 0.95 us: per_device(): now = state_now[0].astype(f32)]
    pallas_call x1, Pallas kernels: 4.64 us -> 2.92 us  [per_device(): pl.pallas_call(functools.partial(before_kernel, slabs, depth, width_x), o...]
  transfers between devices with their start and end apart: 9 -> 9, of which waited for: 2 -> 5; matrix products, arithmetic and copies ran while one was open for 2% -> 2% of each run, Pallas kernels for 11% -> 6%
where the time goes in v2:
time: 134 us; the launch traced here: 132 us
  starting transfers between devices  47.5 us (35%)
  blocking collectives  36.3 us (27%)
  Pallas kernels  22.1 us (16%)
  waiting for transfers between devices  17.8 us (13%)
  local copies, waits for them, and re-layouts  6.5 us (5%)
  between operations  1.47 us (1%)
    all_to_all x1, blocking collectives, per_device(): lax.all_to_all(grad.reshape(groups, width_x, width_y), 'shots', split_axi...  36.3 us
    ppermute x7, starting transfers between devices, shift(): lax.ppermute(x, 'sub', [(i, (i + distance) % count) for i in range(count)])  24.4 us
    all_to_all x1, starting transfers between devices, per_device(): lax.all_to_all(panels.reshape(groups, width_x, width_y), 'shots', split_a...  19.3 us
    all_to_all x1, waiting for transfers between devices, per_device(): lax.all_to_all(owned.reshape(slabs, model_x // slabs, model_y), 'sub', sp...  8.24 us
    pallas_call x1, Pallas kernels, per_device(): pl.pallas_call(functools.partial(main_kernel, slabs, depth, width_x), out...  7.33 us
    ppermute x7, waiting for transfers between devices, shift(): lax.ppermute(x, 'sub', [(i, (i + distance) % count) for i in range(count)])  6.03 us
    unnamed x20, local copies, waits for them, and re-layouts  4.84 us
    pallas_call x1, Pallas kernels, per_device(): pl.pallas_call(functools.partial(receiver_kernel, rec_index.shape[1], acr...  4.5 us
  transfers between devices with their start and end apart: 9, of which 5 were waited for; matrix products, arithmetic and copies ran while one was open for 2% of the time, Pallas kernels for 6%

profile of v2, /device:TPU:24, one launch (start us, length us, event | category | flops | bytes accessed | tf_op | source)
XLA Modules:
  0.0 132.4 jit_solution(966371057600543718)
XLA Ops:
  0.6 0.0 copy-start.3
  0.6 4.3 %first.1 = (f32[2048,128]{1,0:T(8,128)}, f32[512,128]{1,0:T(8,128)}) custom-call(s32[1]{0:T(128)} %bitcast.me_ref, s32[128]{0:T(128)} %ax_ref.3, s32[128]{0:T(128)} %ay_ref.3, f32[512,256]{1,0:T(8,128)} %bitcast.39, bf16[128,4,128]{2,1,0:T(4,128)(2,1)} %bitcast.41, bf16[128,4,128]{2,1,0:T(4,128)(2,1)} %bitcast.42, bf16[128,4,128]{2,1,0:T(4,128)(2,1)} %bitcast.43, ...), custom_call_target="tpu_custom_call" | custom-call | tf_op jit(solution)/shard_map/first/pallas_call | solution.py:388
  5.0 0.0 copy-start.2
  5.0 4.8 %collective-permute-start.4 = (f32[2048,128]{1,0:T(8,128)}, f32[2048,128]{1,0:T(8,128)S(1)}, u32[]{:S(2)}, u32[]{:S(2)}) collective-permute-start(f32[2048,128]{1,0:T(8,128)} %get-tuple-element.17), channel_id=1, source_target_pairs={{0,3},{1,0},{2,1},{3,2},{4,7},{5,4},{6,5},{7,6},{8,11},{9,8},{10,9... | collective-permute-start | bytes 3145736 | tf_op jit(solution)/shard_map/ppermute | solution.py:358
  9.8 1.9 %collective-permute-start.3 = (f32[2048,128]{1,0:T(8,128)}, f32[2048,128]{1,0:T(8,128)S(1)}, u32[]{:S(2)}, u32[]{:S(2)}) collective-permute-start(f32[2048,128]{1,0:T(8,128)} %get-tuple-element.17), channel_id=1, source_target_pairs={{0,1},{1,2},{2,3},{3,0},{4,5},{5,6},{6,7},{7,4},{8,9},{9,10},{10,1... | collective-permute-start | bytes 3145736 | tf_op jit(solution)/shard_map/ppermute | solution.py:358
  11.7 19.3 %all-to-all-start = ((f32[128,4,128]{2,1,0:T(4,128)}), f32[128,4,128]{2,1,0:T(4,128)S(1)}, u32[]{:S(2)}, u32[]{:S(2)}) async-start(f32[128,4,128]{2,1,0:T(4,128)} %bitcast.40), calls=%async_computation | async-start | bytes 524288 | tf_op jit(solution)/shard_map/all_to_all | solution.py:409
  31.0 1.5 %collective-permute-done.4 = f32[2048,128]{1,0:T(8,128)S(1)} collective-permute-done((f32[2048,128]{1,0:T(8,128)}, f32[2048,128]{1,0:T(8,128)S(1)}, u32[]{:S(2)}, u32[]{:S(2)}) %collective-permute-start.4) | collective-permute-done | bytes 1048608 | tf_op jit(solution)/shard_map/ppermute | solution.py:358
  32.5 0.8 slice.25
  33.3 5.5 %collective-permute-start.6 = (f32[1024,128]{1,0:T(8,128)}, f32[1024,128]{1,0:T(8,128)}, u32[]{:S(2)}, u32[]{:S(2)}) collective-permute-start(f32[1024,128]{1,0:T(8,128)} %slice.25), channel_id=1, source_target_pairs={{0,3},{1,0},{2,1},{3,2},{4,7},{5,4},{6,5},{7,6},{8,11},{9,8},{10,9... | collective-permute-start | bytes 1572872 | tf_op jit(solution)/shard_map/ppermute | solution.py:358
  38.8 0.0 collective-permute-done.3
  38.8 0.8 slice.24
  39.7 1.9 %collective-permute-start.5 = (f32[1024,128]{1,0:T(8,128)}, f32[1024,128]{1,0:T(8,128)}, u32[]{:S(2)}, u32[]{:S(2)}) collective-permute-start(f32[1024,128]{1,0:T(8,128)} %slice.24), channel_id=1, source_target_pairs={{0,1},{1,2},{2,3},{3,0},{4,5},{5,6},{6,7},{7,4},{8,9},{9,10},{10,1... | collective-permute-start | bytes 1572872 | tf_op jit(solution)/shard_map/ppermute | solution.py:358
  41.6 0.0 copy-start.4
  41.6 0.7 copy-done.4
  42.3 0.0 copy-start.5
  42.3 0.7 copy-done.5
  43.0 0.0 copy-start.8
  43.0 4.5 %receivers.1 = f32[2048,4,128]{2,1,0:T(4,128)S(1)} custom-call(s32[512]{0:T(512)S(1)} %bitcast.38, f32[3,1,512]{2,1,0:T(1,128)S(1)} %bitcast.37), custom_call_target="tpu_custom_call" | custom-call | tf_op jit(solution)/shard_map/receivers/pallas_call | solution.py:413
  47.5 0.0 copy-start
  47.5 1.9 %copy-done = f32[2048,4,128]{2,1,0:T(4,128)} copy-done((f32[2048,4,128]{2,1,0:T(4,128)}, f32[2048,4,128]{2,1,0:T(4,128)S(1)}, u32[]{:S(2)}) %copy-start) | copy-done | bytes 4194328
  49.4 3.5 %all-to-all-done = f32[128,4,128]{2,1,0:T(4,128)S(1)} async-done(((f32[128,4,128]{2,1,0:T(4,128)}), f32[128,4,128]{2,1,0:T(4,128)S(1)}, u32[]{:S(2)}, u32[]{:S(2)}) %all-to-all-start) | async-done | bytes 262176 | tf_op jit(solution)/shard_map/all_to_all | solution.py:409
  52.9 0.0 copy-start.1
  52.9 4.4 %collective-permute-start.2 = (f32[512,128]{1,0:T(8,128)S(1)}, f32[512,128]{1,0:T(8,128)S(1)}, u32[]{:S(2)}, u32[]{:S(2)}) collective-permute-start(f32[512,128]{1,0:T(8,128)S(1)} %bitcast.29), channel_id=1, source_target_pairs={{0,2},{1,3},{2,0},{3,1},{4,6},{5,7},{6,4},{7,5},{8,10},{9,11},{10,... | collective-permute-start | bytes 786440 | tf_op jit(solution)/shard_map/ppermute | solution.py:358
  57.4 3.0 %collective-permute-start.1 = (f32[512,128]{1,0:T(8,128)S(1)}, f32[512,128]{1,0:T(8,128)S(1)}, u32[]{:S(2)}, u32[]{:S(2)}) collective-permute-start(f32[512,128]{1,0:T(8,128)S(1)} %bitcast.30), channel_id=1, source_target_pairs={{0,3},{1,0},{2,1},{3,2},{4,7},{5,4},{6,5},{7,6},{8,11},{9,8},{10,9... | collective-permute-start | bytes 786440 | tf_op jit(solution)/shard_map/ppermute | solution.py:358
  60.4 2.8 %collective-permute-start = (f32[512,128]{1,0:T(8,128)S(1)}, f32[512,128]{1,0:T(8,128)S(1)}, u32[]{:S(2)}, u32[]{:S(2)}) collective-permute-start(f32[512,128]{1,0:T(8,128)S(1)} %bitcast.31), channel_id=1, source_target_pairs={{0,1},{1,2},{2,3},{3,0},{4,5},{5,6},{6,7},{7,4},{8,9},{9,10},{10,1... | collective-permute-start | bytes 786440 | tf_op jit(solution)/shard_map/ppermute | solution.py:358
  63.9 0.0 collective-permute-done.6
  63.9 0.0 collective-permute-done.5
  63.9 0.0 copy-done.3
  63.9 0.0 copy-done.2
  63.9 2.9 %before.1 = (f32[24,128,128]{2,1,0:T(8,128)S(1)}, f32[16,128,128]{2,1,0:T(8,128)S(1)}, f32[16,128,128]{2,1,0:T(8,128)S(1)}, f32[16,128,128]{2,1,0:T(8,128)S(1)}, f32[16,128,128]{2,1,0:T(8,128)S(1)}) custom-call(s32[1]{0:T(128)} %bitcast.me_ref, f32[16,128,128]{2,1,0:T(8,128)S(1)} %bitcast.28, f32[16,128,128]{2,1,0:T(8,128)S(1)} %bitcast.27, ...), custom_call_target="tpu_custom_call" | custom-call | tf_op jit(solution)/shard_map/before/pallas_call | solution.py:424
  66.8 0.0 collective-permute-done.2.far_ref
  66.9 4.3 %collective-permute-done.1.right_ref = f32[512,128]{1,0:T(8,128)S(1)} collective-permute-done((f32[512,128]{1,0:T(8,128)S(1)}, f32[512,128]{1,0:T(8,128)S(1)}, u32[]{:S(2)}, u32[]{:S(2)}) %collective-permute-start.1) | collective-permute-done | bytes 262176 | tf_op jit(solution)/shard_map/ppermute | solution.py:358
  71.1 0.3 collective-permute-done.left_ref
  71.4 0.0 copy-done.8
  71.4 0.0 copy-done.1
  71.4 0.0 copy-start.6
  71.4 0.0 copy-start.7
  71.4 7.3 %window.1 = (f32[512,128]{1,0:T(8,128)S(1)}, bf16[4,128,128]{2,1,0:T(8,128)(2,1)S(1)}, bf16[4,128,128]{2,1,0:T(8,128)(2,1)S(1)}) custom-call(s32[1]{0:T(128)} %bitcast.me_ref, s32[1]{0:T(128)S(6)} %copy.17.source_ref, f32[1,3]{1,0:T(1,128)S(1)} %copy-done.8, f32[512,128]{1,0:T(8,128)S(1)} %bitcast.32, f32[512,128]{1,0:T(8,128)S(1)} %collective-permute-done.left_ref, ...), custom_call_target="tpu_custom_call" | custom-call | tf_op jit(solution)/shard_map/window/pallas_call | solution.py:440
  78.7 36.3 %all_to_all.15 = f32[128,4,128]{2,1,0:T(4,128)S(1)} all-to-all(f32[128,4,128]{2,1,0:T(4,128)S(1)} %bitcast.34), channel_id=1, replica_groups=mesh['shots'=128,'sub'=4] {'shots'}, dimensions={0} | all-to-all | bytes 524288 | tf_op jit(solution)/shard_map/all_to_all | solution.py:466
  115.1 0.0 copy-done.6
  115.1 0.0 copy-done.7
  115.1 3.0 %spread.1 = f32[512,256]{1,0:T(8,128)} custom-call(s32[1]{0:T(128)} %bitcast.me_ref, s32[128]{0:T(128)S(1)} %copy-done.6, s32[128]{0:T(128)S(1)} %copy-done.7, f32[512,128]{1,0:T(8,128)S(1)} %bitcast.33), custom_call_target="tpu_custom_call" | custom-call | tf_op jit(solution)/shard_map/spread/pallas_call | solution.py:469
  118.1 3.8 %all-to-all-start.2 = ((f32[4,128,256]{2,1,0:T(8,128)}), f32[4,128,256]{2,1,0:T(8,128)S(1)}, u32[]{:S(2)}, u32[]{:S(2)}) async-start(f32[4,128,256]{2,1,0:T(8,128)} %bitcast.18), calls=%async_computation.2 | async-start | bytes 1048576 | tf_op jit(solution)/shard_map/all_to_all | solution.py:478
  121.9 0.8 copy.15
  122.7 0.8 copy.16
  123.5 8.2 %all-to-all-done.2 = f32[4,128,256]{2,1,0:T(8,128)S(1)} async-done(((f32[4,128,256]{2,1,0:T(8,128)}), f32[4,128,256]{2,1,0:T(8,128)S(1)}, u32[]{:S(2)}, u32[]{:S(2)}) %all-to-all-start.2) | async-done | bytes 524320 | tf_op jit(solution)/shard_map/all_to_all | solution.py:478
  131.7 0.7 slice_add_fusion
Async XLA Ops:
  0.6 63.3 %copy-start.3 = (bf16[128,128]{1,0:T(8,128)(2,1)S(1)}, bf16[128,128]{1,0:T(8,128)(2,1)}, u32[]{:S(2)}) copy-start(bf16[128,128]{1,0:T(8,128)(2,1)} %constant.6.clone.band_ref) | copy-start | bytes 98308
  5.0 58.9 %copy-start.2 = (f32[2048,128]{1,0:T(8,128)S(1)}, f32[2048,128]{1,0:T(8,128)}, u32[]{:S(2)}) copy-start(f32[2048,128]{1,0:T(8,128)} %get-tuple-element.17) | copy-start | bytes 3145732
  5.0 27.5 %collective-permute-start.4 = (f32[2048,128]{1,0:T(8,128)}, f32[2048,128]{1,0:T(8,128)S(1)}, u32[]{:S(2)}, u32[]{:S(2)}) collective-permute-start(f32[2048,128]{1,0:T(8,128)} %get-tuple-element.17), channel_id=1, source_target_pairs={{0,3},{1,0},{2,1},{3,2},{4,7},{5,4},{6,5},{7,6},{8,11},{9,8},{10,9... | collective-permute-start | bytes 3145736 | tf_op jit(solution)/shard_map/ppermute | solution.py:358
  9.8 29.0 %collective-permute-start.3 = (f32[2048,128]{1,0:T(8,128)}, f32[2048,128]{1,0:T(8,128)S(1)}, u32[]{:S(2)}, u32[]{:S(2)}) collective-permute-start(f32[2048,128]{1,0:T(8,128)} %get-tuple-element.17), channel_id=1, source_target_pairs={{0,1},{1,2},{2,3},{3,0},{4,5},{5,6},{6,7},{7,4},{8,9},{9,10},{10,1... | collective-permute-start | bytes 3145736 | tf_op jit(solution)/shard_map/ppermute | solution.py:358
  11.7 41.2 %all-to-all-start = ((f32[128,4,128]{2,1,0:T(4,128)}), f32[128,4,128]{2,1,0:T(4,128)S(1)}, u32[]{:S(2)}, u32[]{:S(2)}) async-start(f32[128,4,128]{2,1,0:T(4,128)} %bitcast.40), calls=%async_computation | async-start | bytes 524288 | tf_op jit(solution)/shard_map/all_to_all | solution.py:409
  33.3 30.6 %collective-permute-start.6 = (f32[1024,128]{1,0:T(8,128)}, f32[1024,128]{1,0:T(8,128)}, u32[]{:S(2)}, u32[]{:S(2)}) collective-permute-start(f32[1024,128]{1,0:T(8,128)} %slice.25), channel_id=1, source_target_pairs={{0,3},{1,0},{2,1},{3,2},{4,7},{5,4},{6,5},{7,6},{8,11},{9,8},{10,9... | collective-permute-start | bytes 1572872 | tf_op jit(solution)/shard_map/ppermute | solution.py:358
  39.7 24.2 %collective-permute-start.5 = (f32[1024,128]{1,0:T(8,128)}, f32[1024,128]{1,0:T(8,128)}, u32[]{:S(2)}, u32[]{:S(2)}) collective-permute-start(f32[1024,128]{1,0:T(8,128)} %slice.24), channel_id=1, source_target_pairs={{0,1},{1,2},{2,3},{3,0},{4,5},{5,6},{6,7},{7,4},{8,9},{9,10},{10,1... | collective-permute-start | bytes 1572872 | tf_op jit(solution)/shard_map/ppermute | solution.py:358
  41.6 0.7 copy-start.4
  42.3 0.7 copy-start.5
  43.0 28.4 %copy-start.8 = (f32[1,3]{1,0:T(1,128)S(1)}, f32[1,3]{1,0:T(1,128)}, u32[]{:S(2)}) copy-start(f32[1,3]{1,0:T(1,128)} %wave_ref.1) | copy-start | bytes 40
  47.5 1.9 %copy-start = (f32[2048,4,128]{2,1,0:T(4,128)}, f32[2048,4,128]{2,1,0:T(4,128)S(1)}, u32[]{:S(2)}) copy-start(f32[2048,4,128]{2,1,0:T(4,128)S(1)} %receivers.1) | copy-start | bytes 12582916
  52.9 18.5 %copy-start.1 = (f32[2048,4,128]{2,1,0:T(4,128)S(1)}, f32[2048,4,128]{2,1,0:T(4,128)}, u32[]{:S(2)}) copy-start(f32[2048,4,128]{2,1,0:T(4,128)} %copy-done) | copy-start | bytes 12582916
  52.9 13.9 %collective-permute-start.2 = (f32[512,128]{1,0:T(8,128)S(1)}, f32[512,128]{1,0:T(8,128)S(1)}, u32[]{:S(2)}, u32[]{:S(2)}) collective-permute-start(f32[512,128]{1,0:T(8,128)S(1)} %bitcast.29), channel_id=1, source_target_pairs={{0,2},{1,3},{2,0},{3,1},{4,6},{5,7},{6,4},{7,5},{8,10},{9,11},{10,... | collective-permute-start | bytes 786440 | tf_op jit(solution)/shard_map/ppermute | solution.py:358
  57.4 13.7 %collective-permute-start.1 = (f32[512,128]{1,0:T(8,128)S(1)}, f32[512,128]{1,0:T(8,128)S(1)}, u32[]{:S(2)}, u32[]{:S(2)}) collective-permute-start(f32[512,128]{1,0:T(8,128)S(1)} %bitcast.30), channel_id=1, source_target_pairs={{0,3},{1,0},{2,1},{3,2},{4,7},{5,4},{6,5},{7,6},{8,11},{9,8},{10,9... | collective-permute-start | bytes 786440 | tf_op jit(solution)/shard_map/ppermute | solution.py:358
  60.4 11.0 %collective-permute-start = (f32[512,128]{1,0:T(8,128)S(1)}, f32[512,128]{1,0:T(8,128)S(1)}, u32[]{:S(2)}, u32[]{:S(2)}) collective-permute-start(f32[512,128]{1,0:T(8,128)S(1)} %bitcast.31), channel_id=1, source_target_pairs={{0,1},{1,2},{2,3},{3,0},{4,5},{5,6},{6,7},{7,4},{8,9},{9,10},{10,1... | collective-permute-start | bytes 786440 | tf_op jit(solution)/shard_map/ppermute | solution.py:358
  71.4 43.7 %copy-start.6 = (s32[128]{0:T(128)S(1)}, s32[128]{0:T(128)}, u32[]{:S(2)}) copy-start(s32[128]{0:T(128)} %ax_ref.3) | copy-start | bytes 1540
  71.4 43.7 %copy-start.7 = (s32[128]{0:T(128)S(1)}, s32[128]{0:T(128)}, u32[]{:S(2)}) copy-start(s32[128]{0:T(128)} %ay_ref.3) | copy-start | bytes 1540
  118.1 13.6 %all-to-all-start.2 = ((f32[4,128,256]{2,1,0:T(8,128)}), f32[4,128,256]{2,1,0:T(8,128)S(1)}, u32[]{:S(2)}, u32[]{:S(2)}) async-start(f32[4,128,256]{2,1,0:T(8,128)} %bitcast.18), calls=%async_computation.2 | async-start | bytes 1048576 | tf_op jit(solution)/shard_map/all_to_all | solution.py:478

commit v3 on v2

--- a/solution.py
+++ b/solution.py
@@ -30,19 +30,26 @@
 
 
 ROWS = 16
+GROUP = 2
 
 
 def along(ref, x, count, band_ref, part_ref):
     weights = band_ref[...]
     twice_down = jnp.concatenate([weights, weights], axis=0)
     twice_across = jnp.concatenate([weights, weights], axis=1)
-    for index in range(count):
-        centre = ref[x + REACH + index]
-        high = centre.astype(jnp.bfloat16)
-        low = (centre - high.astype(jnp.float32)).astype(jnp.bfloat16)
-        along_y = jnp.dot(jnp.concatenate([high, low], axis=1), twice_down, preferred_element_type=jnp.float32)
-        along_z = jnp.dot(twice_across, jnp.concatenate([high, low], axis=0), preferred_element_type=jnp.float32)
-        part_ref[index] = along_y + along_z
+    for index in range(0, count, 2):
+        highs, lows = [], []
+        for slice_x in (x + REACH + index, x + REACH + index + 1):
+            centre = ref[slice_x]
+            highs.append(centre.astype(jnp.bfloat16))
+            lows.append((centre - highs[-1].astype(jnp.float32)).astype(jnp.bfloat16))
+        beside = [jnp.concatenate(pair, axis=1) for pair in zip(highs, lows)]
+        along_y = jnp.dot(jnp.concatenate(beside, axis=0), twice_down, preferred_element_type=jnp.float32)
+        above = jnp.concatenate([jnp.concatenate(highs, axis=1), jnp.concatenate(lows, axis=1)], axis=0)
+        along_z = jnp.dot(twice_across, above, preferred_element_type=jnp.float32)
+        size = weights.shape[0]
+        part_ref[index] = along_y[:size] + along_z[:, :size]
+        part_ref[index + 1] = along_y[size:] + along_z[:, size:]
 
 
 def laplace(ref, x, count, rows, part_ref):
@@ -62,7 +69,7 @@
         step(pl.ds(pl.multiple_of(index * ROWS, ROWS), ROWS), pl.multiple_of(index * ROWS, ROWS))
         return carry
 
-    lax.fori_loop(0, depth // ROWS, body, 0, unroll=2)
+    lax.fori_loop(0, depth // ROWS, body, 0, unroll=8)
 
 
 def spread_kernel(shots, width_x, me_ref, ax_ref, ay_ref, in_ref, out_ref, near_ref, far_ref):
@@ -93,29 +100,44 @@
     return lax.shift_right_logical(row, shift_x), row & (across - 1), flat & (width_y - 1)
 
 
-def receiver_kernel(count, across, depth, index_ref, seen_ref, out_ref):
-    width_y = out_ref.shape[2]
+def receiver_kernel(count, across, depth, index_hbm, seen_hbm, out_ref, index_ref, seen_ref, sems):
+    width_y = out_ref.shape[1]
+    load_index = pltpu.make_async_copy(index_hbm, index_ref, sems.at[0])
+    load_seen = pltpu.make_async_copy(seen_hbm, seen_ref, sems.at[1])
+    load_index.start()
+    load_seen.start()
     out_ref[...] = jnp.zeros_like(out_ref)
-    shape = out_ref.shape[1:]
+    load_index.wait()
+    load_seen.wait()
+    shape = (4, width_y)
     lane = lax.broadcasted_iota(jnp.int32, shape, 1)
     line = lax.broadcasted_iota(jnp.int32, shape, 0)
 
-    def body(receiver, carry):
-        cell_z, cell_x, cell_y = cell(index_ref[receiver], across, width_y)
-        value = jnp.where(line == 1, seen_ref[0, 0, receiver], 1.0)
-        value = jnp.where(line == 2, seen_ref[1, 0, receiver], value)
-        value = jnp.where(line == 3, seen_ref[2, 0, receiver], value)
-        row = cell_x * depth + cell_z
-        out_ref[row] = out_ref[row] + jnp.where(lane == cell_y, value, 0.0)
+    def body(group, carry):
+        starts, sums = [], []
+        for member in range(GROUP):
+            receiver = group * GROUP + member
+            cell_z, cell_x, cell_y = cell(index_ref[0, receiver], across, width_y)
+            value = jnp.where(line == 1, seen_ref[0, 0, receiver], 1.0)
+            value = jnp.where(line == 2, seen_ref[1, 0, receiver], value)
+            value = jnp.where(line == 3, seen_ref[2, 0, receiver], value)
+            start = pl.multiple_of((cell_x * depth + cell_z) * 4, 4)
+            tile = out_ref[pl.ds(start, 4), :]
+            for earlier, total in zip(starts, sums):
+                tile = jnp.where(earlier == start, total, tile)
+            starts.append(start)
+            sums.append(tile + jnp.where(lane == cell_y, value, 0.0))
+        for start, total in zip(starts, sums):
+            out_ref[pl.ds(start, 4), :] = total
         return carry
 
-    lax.fori_loop(0, count, body, 0, unroll=4)
+    lax.fori_loop(0, count // GROUP, body, 0, unroll=4)
 
 
 def first_kernel(
-    shots, depth, width_x, me_ref, ax_ref, ay_ref, model_hbm, before_hbm, now_hbm, later_hbm, latest_hbm,
+    shots, depth, width_x, me_ref, ax_hbm, ay_hbm, model_hbm, before_hbm, now_hbm, later_hbm, latest_hbm,
     fields_hbm, panels_hbm,
-    near_ref, far_ref, before_ref, now_ref, later_ref, latest_ref, turn_ref, fields_ref, panels_ref, in_sems, out_sems,
+    near_ref, far_ref, before_ref, now_ref, later_ref, latest_ref, turn_ref, fields_ref, panels_ref, ax_ref, ay_ref, in_sems, out_sems,
 ):
     block = depth * width_x
     width_y = panels_ref.shape[1]
@@ -126,6 +148,8 @@
         (latest_hbm, latest_ref),
         (model_hbm.at[:, :width_y], near_ref),
         (model_hbm.at[:, width_y:], far_ref),
+        (ax_hbm, ax_ref),
+        (ay_hbm, ay_ref),
     )
     loads = [pltpu.make_async_copy(source, ref, in_sems.at[k]) for k, (source, ref) in enumerate(pairs)]
     for load in loads:
@@ -223,14 +247,16 @@
 
 def main_kernel(
     slabs, depth, width_x, me_ref, source_ref, wave_ref, own_ref, left_ref, right_ref, far_ref,
-    start_ref, push_ref, later_ref, back_ref, curve_ref, extra_ref, band_ref,
+    start_ref, push_ref, later_ref, back_ref, curve_ref, extra_hbm, band_ref,
     grad_ref, first_ref, second_ref,
     speed_ref, one_ref, two_ref, scaled_ref, again_ref, curve_one_ref, lam_ref, lam_two_ref, sum_ref, mark_ref,
-    part_ref, other_ref,
+    part_ref, other_ref, extra_ref, extra_sem,
 ):
     me = me_ref[0]
     across = slabs * width_x
     width_y = mark_ref.shape[1]
+    load_extra = pltpu.make_async_copy(extra_hbm, extra_ref, extra_sem)
+    load_extra.start()
     for distance, ref in ((0, own_ref), (slabs - 1, left_ref), (1, right_ref), (2, far_ref)):
         base = lax.rem(me + distance, slabs) * width_x
         for row in range(width_x):
@@ -245,6 +271,12 @@
     spot_y = lax.broadcasted_iota(jnp.int32, (depth, width_y), 1) == source_y
     mark_ref[...] = jnp.where(spot_z & spot_y, 1.0, 0.0)
 
+    def add_source(ref, step):
+        row = pl.ds(source_z, 1)
+        lane = lax.broadcasted_iota(jnp.int32, (1, width_y), 1)
+        pulse = jnp.where(lane == source_y, wave_ref[0, step], 0.0)
+        ref[source_x + REACH, row, :] = ref[source_x + REACH, row, :] + pulse
+
     def pulse(x, step, rows):
         return mark_ref[rows, :] * jnp.where(x == source_x, wave_ref[0, step], 0.0)
 
@@ -267,13 +299,14 @@
                 here = x + here
                 speed = speed_ref[here, rows, :]
                 one_ref[here + REACH, rows, :] = (
-                    push_ref[here, rows, :] + speed * curve_ref[here, rows, :] + pulse(here, 0, rows)
+                    push_ref[here, rows, :] + speed * curve_ref[here, rows, :]
                 )
                 scaled_ref[here + REACH, rows, :] = speed * later_ref[here, rows, :]
 
         over_rows(depth, step)
 
     by_slabs(step_one, across)
+    add_source(one_ref, 0)
 
     def step_two(x):
         along(one_ref, x, width_x, band_ref, part_ref)
@@ -286,12 +319,12 @@
                     2.0 * one_ref[here + REACH, rows, :]
                     - start_ref[here + REACH, rows, :]
                     + speed_ref[here, rows, :] * bend
-                    + pulse(here, 1, rows)
                 )
 
         over_rows(depth, step)
 
     by_slabs(step_two, across)
+    add_source(two_ref, 1)
 
     def back_three(x):
         along(two_ref, x, width_x, band_ref, part_ref)
@@ -317,6 +350,7 @@
 
         over_rows(depth, step)
 
+    load_extra.wait()
     by_slabs(back_three, 2 * REACH)
 
     def back_two(x):
@@ -388,7 +422,7 @@
     fields, panels = pl.pallas_call(
         functools.partial(first_kernel, groups, depth, width_x),
         out_shape=[shape(4 * block, width_y), shape(groups * width_x, width_y)],
-        in_specs=[SMEM] * 3 + [HBM] * 5,
+        in_specs=[SMEM] + [HBM] * 7,
         out_specs=[HBM] * 2,
         scratch_shapes=[pltpu.VMEM((model_x, width_y), f32)] * 2
         + [state] * 4
@@ -396,28 +430,34 @@
             pltpu.VMEM((depth, width_x, width_y), f32),
             pltpu.VMEM((4 * block, width_y), f32),
             pltpu.VMEM((groups * width_x, width_y), f32),
-            pltpu.SemaphoreType.DMA((6,)),
+            pltpu.SMEM((groups,), jnp.int32),
+            pltpu.SMEM((groups,), jnp.int32),
+            pltpu.SemaphoreType.DMA((8,)),
             pltpu.SemaphoreType.DMA((2,)),
         ],
         name="first",
     )(me, anchor_x, anchor_y, model[0], state_before[0], state_now[0], adjoint_later[0], adjoint_latest[0])
     left = shift(fields, 1)
     right = shift(fields, -1)
+    extra = pl.pallas_call(
+        functools.partial(receiver_kernel, rec_index.shape[1], across, depth),
+        out_shape=shape(across * depth * 4, width_y),
+        in_specs=[HBM, HBM],
+        out_specs=VMEM,
+        scratch_shapes=[
+            pltpu.SMEM((1, rec_index.shape[1]), jnp.int32),
+            pltpu.SMEM((STEPS, 1, rec_index.shape[1]), f32),
+            pltpu.SemaphoreType.DMA((2,)),
+        ],
+        name="receivers",
+    )(rec_index, jnp.transpose(observed, (1, 0, 2)))
+
     far_a = shift(left[: 2 * block], 1)
     far_b = shift(right[2 * block :], -1)
 
     speed = lax.all_to_all(
         panels.reshape(groups, width_x, width_y), "shots", split_axis=0, concat_axis=0, tiled=True
     ).reshape(block, width_y)
-
-    extra = pl.pallas_call(
-        functools.partial(receiver_kernel, rec_index.shape[1], across, depth),
-        out_shape=shape(across * depth, 4, width_y),
-        in_specs=[SMEM, SMEM],
-        out_specs=VMEM,
-        compiler_params=PARAMS,
-        name="receivers",
-    )(rec_index[0], jnp.transpose(observed, (1, 0, 2))).reshape(across * depth * 4, width_y)
 
     whole = (across, depth, width_y)
     padded = (across + 2 * REACH, depth, width_y)
@@ -431,16 +471,15 @@
         name="before",
     )(me, *(piece.reshape(-1, depth, width_y) for piece in (fields, left, right, far_a, far_b)), weights)
 
-    speed, extra = lax.optimization_barrier((speed, extra))
+    speed_far = shift(speed, 2)
+    speed_right = shift(speed, -1)
     speed_left = shift(speed, 1)
-    speed_right = shift(speed, -1)
-    speed_far = shift(speed, 2)
 
     slab = jax.ShapeDtypeStruct((width_x, depth, width_y), jnp.bfloat16)
     grad, first, second = pl.pallas_call(
         functools.partial(main_kernel, slabs, depth, width_x),
         out_shape=[shape(block, width_y), slab, slab],
-        in_specs=[SMEM] * 3 + [VMEM] * 11,
+        in_specs=[SMEM] * 3 + [VMEM] * 9 + [HBM, VMEM],
         out_specs=[VMEM] * 3,
         scratch_shapes=[
             pltpu.VMEM(whole, f32),
@@ -455,6 +494,8 @@
             pltpu.VMEM((depth, width_y), f32),
             pltpu.VMEM((width_x, depth, width_y), f32),
             pltpu.VMEM((width_x, depth, width_y), f32),
+            pltpu.VMEM((across * depth * 4, width_y), f32),
+            pltpu.SemaphoreType.DMA,
         ],
         compiler_params=PARAMS,
         name="window",

time: 134 us -> 132 us (0.985)
  waiting for transfers between devices: 17.8 us -> 21.3 us
  local copies, waits for them, and re-layouts: 6.5 us -> 3.21 us
    all_to_all x1, waiting for transfers between devices: 3.51 us -> 11.3 us  [per_device(): lax.all_to_all(panels.reshape(groups, width_x, width_y), 'shots', split_a...]
    ppermute x7, waiting for transfers between devices: 6.03 us -> 1.5 us  [shift(): lax.ppermute(x, 'sub', [(i, (i + distance) % count) for i in range(count)])]
    unnamed x20 -> x14, local copies, waits for them, and re-layouts: 4.84 us -> 1.55 us
    pallas_call x1, Pallas kernels: 4.5 us -> 6.09 us  [per_device(): pl.pallas_call(functools.partial(receiver_kernel, rec_index.shape[1], acr...]
  transfers between devices with their start and end apart: 9 -> 9, of which waited for: 5 -> 3; matrix products, arithmetic and copies ran while one was open for 2% -> 2% of each run, Pallas kernels for 6% -> 7%
where the time goes in v3:
time: 132 us; the launch traced here: 131 us
  starting transfers between devices  46.9 us (36%)
  blocking collectives  35.5 us (27%)
  Pallas kernels  21.9 us (17%)
  waiting for transfers between devices  21.3 us (16%)
  local copies, waits for them, and re-layouts  3.21 us (2%)
  between operations  1.52 us (1%)
    all_to_all x1, blocking collectives, per_device(): lax.all_to_all(grad.reshape(groups, width_x, width_y), 'shots', split_axi...  35.5 us
    ppermute x7, starting transfers between devices, shift(): lax.ppermute(x, 'sub', [(i, (i + distance) % count) for i in range(count)])  24.1 us
    all_to_all x1, starting transfers between devices, per_device(): lax.all_to_all(panels.reshape(groups, width_x, width_y), 'shots', split_a...  19.3 us
    all_to_all x1, waiting for transfers between devices, per_device(): lax.all_to_all(panels.reshape(groups, width_x, width_y), 'shots', split_a...  11.3 us
    all_to_all x1, waiting for transfers between devices, per_device(): lax.all_to_all(owned.reshape(slabs, model_x // slabs, model_y), 'sub', sp...  8.48 us
    pallas_call x1, Pallas kernels, per_device(): pl.pallas_call(functools.partial(main_kernel, slabs, depth, width_x), out...  6.66 us
    pallas_call x1, Pallas kernels, per_device(): pl.pallas_call(functools.partial(receiver_kernel, rec_index.shape[1], acr...  6.09 us
    pallas_call x1, Pallas kernels, per_device(): pl.pallas_call(functools.partial(first_kernel, groups, depth, width_x), o...  3.69 us
  transfers between devices with their start and end apart: 9, of which 3 were waited for; matrix products, arithmetic and copies ran while one was open for 2% of the time, Pallas kernels for 7%

profile of v3, /device:TPU:24, one launch (start us, length us, event | category | flops | bytes accessed | tf_op | source)
XLA Modules:
  0.0 131.1 jit_solution(3060058867229407204)
XLA Ops:
  0.6 0.0 copy-start.2
  0.6 3.7 %first.1 = (f32[2048,128]{1,0:T(8,128)}, f32[512,128]{1,0:T(8,128)}) custom-call(s32[1]{0:T(128)} %bitcast.me_ref, s32[128]{0:T(128)} %ax_ref.1, s32[128]{0:T(128)} %ay_ref.1, f32[512,256]{1,0:T(8,128)} %bitcast.34, bf16[128,4,128]{2,1,0:T(4,128)(2,1)} %bitcast.36, bf16[128,4,128]{2,1,0:T(4,128)(2,1)} %bitcast.37, bf16[128,4,128]{2,1,0:T(4,128)(2,1)} %bitcast.38, ...), custom_call_target="tpu_custom_call" | custom-call | tf_op jit(solution)/shard_map/first/pallas_call | solution.py:422
  4.3 0.0 copy-start.1
  4.4 4.8 %collective-permute-start.4 = (f32[2048,128]{1,0:T(8,128)}, f32[2048,128]{1,0:T(8,128)S(1)}, u32[]{:S(2)}, u32[]{:S(2)}) collective-permute-start(f32[2048,128]{1,0:T(8,128)} %get-tuple-element.14), channel_id=1, source_target_pairs={{0,3},{1,0},{2,1},{3,2},{4,7},{5,4},{6,5},{7,6},{8,11},{9,8},{10,9... | collective-permute-start | bytes 3145736 | tf_op jit(solution)/shard_map/ppermute | solution.py:392
  9.2 1.9 %collective-permute-start.3 = (f32[2048,128]{1,0:T(8,128)}, f32[2048,128]{1,0:T(8,128)S(1)}, u32[]{:S(2)}, u32[]{:S(2)}) collective-permute-start(f32[2048,128]{1,0:T(8,128)} %get-tuple-element.14), channel_id=1, source_target_pairs={{0,1},{1,2},{2,3},{3,0},{4,5},{5,6},{6,7},{7,4},{8,9},{9,10},{10,1... | collective-permute-start | bytes 3145736 | tf_op jit(solution)/shard_map/ppermute | solution.py:392
  11.1 19.3 %all-to-all-start = ((f32[128,4,128]{2,1,0:T(4,128)}), f32[128,4,128]{2,1,0:T(4,128)S(1)}, u32[]{:S(2)}, u32[]{:S(2)}) async-start(f32[128,4,128]{2,1,0:T(4,128)} %bitcast.35), calls=%async_computation | async-start | bytes 524288 | tf_op jit(solution)/shard_map/all_to_all | solution.py:458
  30.4 1.5 %collective-permute-done.4 = f32[2048,128]{1,0:T(8,128)S(1)} collective-permute-done((f32[2048,128]{1,0:T(8,128)}, f32[2048,128]{1,0:T(8,128)S(1)}, u32[]{:S(2)}, u32[]{:S(2)}) %collective-permute-start.4) | collective-permute-done | bytes 1048608 | tf_op jit(solution)/shard_map/ppermute | solution.py:392
  31.9 0.8 slice.25
  32.7 5.5 %collective-permute-start.6 = (f32[1024,128]{1,0:T(8,128)}, f32[1024,128]{1,0:T(8,128)}, u32[]{:S(2)}, u32[]{:S(2)}) collective-permute-start(f32[1024,128]{1,0:T(8,128)} %slice.25), channel_id=1, source_target_pairs={{0,3},{1,0},{2,1},{3,2},{4,7},{5,4},{6,5},{7,6},{8,11},{9,8},{10,9... | collective-permute-start | bytes 1572872 | tf_op jit(solution)/shard_map/ppermute | solution.py:392
  38.2 0.0 collective-permute-done.3
  38.2 0.8 slice.24
  39.0 1.9 %collective-permute-start.5 = (f32[1024,128]{1,0:T(8,128)}, f32[1024,128]{1,0:T(8,128)}, u32[]{:S(2)}, u32[]{:S(2)}) collective-permute-start(f32[1024,128]{1,0:T(8,128)} %slice.24), channel_id=1, source_target_pairs={{0,1},{1,2},{2,3},{3,0},{4,5},{5,6},{6,7},{7,4},{8,9},{9,10},{10,1... | collective-permute-start | bytes 1572872 | tf_op jit(solution)/shard_map/ppermute | solution.py:392
  41.0 11.3 %all-to-all-done = f32[128,4,128]{2,1,0:T(4,128)S(1)} async-done(((f32[128,4,128]{2,1,0:T(4,128)}), f32[128,4,128]{2,1,0:T(4,128)S(1)}, u32[]{:S(2)}, u32[]{:S(2)}) %all-to-all-start) | async-done | bytes 262176 | tf_op jit(solution)/shard_map/all_to_all | solution.py:458
  52.3 4.2 %collective-permute-start.2 = (f32[512,128]{1,0:T(8,128)S(1)}, f32[512,128]{1,0:T(8,128)}, u32[]{:S(2)}, u32[]{:S(2)}) collective-permute-start(f32[512,128]{1,0:T(8,128)S(1)} %bitcast.26), channel_id=1, source_target_pairs={{0,2},{1,3},{2,0},{3,1},{4,6},{5,7},{6,4},{7,5},{8,10},{9,11},{10,... | collective-permute-start | bytes 786440 | tf_op jit(solution)/shard_map/ppermute | solution.py:392
  56.5 3.0 %collective-permute-start.1 = (f32[512,128]{1,0:T(8,128)S(1)}, f32[512,128]{1,0:T(8,128)}, u32[]{:S(2)}, u32[]{:S(2)}) collective-permute-start(f32[512,128]{1,0:T(8,128)S(1)} %bitcast.27), channel_id=1, source_target_pairs={{0,3},{1,0},{2,1},{3,2},{4,7},{5,4},{6,5},{7,6},{8,11},{9,8},{10,9... | collective-permute-start | bytes 786440 | tf_op jit(solution)/shard_map/ppermute | solution.py:392
  59.5 2.8 %collective-permute-start = (f32[512,128]{1,0:T(8,128)S(1)}, f32[512,128]{1,0:T(8,128)}, u32[]{:S(2)}, u32[]{:S(2)}) collective-permute-start(f32[512,128]{1,0:T(8,128)S(1)} %bitcast.28), channel_id=1, source_target_pairs={{0,1},{1,2},{2,3},{3,0},{4,5},{5,6},{6,7},{7,4},{8,9},{9,10},{10,1... | collective-permute-start | bytes 786440 | tf_op jit(solution)/shard_map/ppermute | solution.py:392
  63.0 0.0 copy-start.5
  63.0 6.1 %receivers.1.extra_hbm = f32[8192,128]{1,0:T(8,128)} custom-call(s32[1,512]{1,0:T(1,128)} %index_hbm.1, f32[3,1,512]{2,1,0:T(1,128)} %bitcast.40), custom_call_target="tpu_custom_call" | custom-call | tf_op jit(solution)/shard_map/receivers/pallas_call | solution.py:442
  69.1 0.0 copy-start
  69.1 0.0 collective-permute-done.6
  69.1 0.0 collective-permute-done.5
  69.1 0.0 copy-done.2
  69.1 0.0 copy-done.1
  69.2 2.5 %before.1 = (f32[24,128,128]{2,1,0:T(8,128)S(1)}, f32[16,128,128]{2,1,0:T(8,128)S(1)}, f32[16,128,128]{2,1,0:T(8,128)S(1)}, f32[16,128,128]{2,1,0:T(8,128)S(1)}, f32[16,128,128]{2,1,0:T(8,128)S(1)}) custom-call(s32[1]{0:T(128)} %bitcast.me_ref, f32[16,128,128]{2,1,0:T(8,128)S(1)} %bitcast.25, f32[16,128,128]{2,1,0:T(8,128)S(1)} %bitcast.24, ...), custom_call_target="tpu_custom_call" | custom-call | tf_op jit(solution)/shard_map/before/pallas_call | solution.py:464
  71.6 0.0 collective-permute-done.2.far_ref
  71.6 0.0 collective-permute-done.1.right_ref
  71.7 0.0 collective-permute-done.left_ref
  71.7 0.0 copy-done.5
  71.7 0.0 copy-done
  71.7 0.0 copy-start.3
  71.7 0.0 copy-start.4
  71.7 6.7 %window.1 = (f32[512,128]{1,0:T(8,128)S(1)}, bf16[4,128,128]{2,1,0:T(8,128)(2,1)S(1)}, bf16[4,128,128]{2,1,0:T(8,128)(2,1)S(1)}) custom-call(s32[1]{0:T(128)} %bitcast.me_ref, s32[1]{0:T(128)S(6)} %copy.17.source_ref, f32[1,3]{1,0:T(1,128)S(1)} %copy-done.5, f32[512,128]{1,0:T(8,128)S(1)} %bitcast.29, f32[512,128]{1,0:T(8,128)} %collective-permute-done.left_ref, ...), custom_call_target="tpu_custom_call" | custom-call | tf_op jit(solution)/shard_map/window/pallas_call | solution.py:479
  78.4 35.5 %all_to_all.15 = f32[128,4,128]{2,1,0:T(4,128)S(1)} all-to-all(f32[128,4,128]{2,1,0:T(4,128)S(1)} %bitcast.31), channel_id=1, replica_groups=mesh['shots'=128,'sub'=4] {'shots'}, dimensions={0} | all-to-all | bytes 524288 | tf_op jit(solution)/shard_map/all_to_all | solution.py:507
  113.9 0.0 copy-done.3
  113.9 0.0 copy-done.4
  113.9 3.0 %spread.1 = f32[512,256]{1,0:T(8,128)} custom-call(s32[1]{0:T(128)} %bitcast.me_ref, s32[128]{0:T(128)S(1)} %copy-done.3, s32[128]{0:T(128)S(1)} %copy-done.4, f32[512,128]{1,0:T(8,128)S(1)} %bitcast.30), custom_call_target="tpu_custom_call" | custom-call | tf_op jit(solution)/shard_map/spread/pallas_call | solution.py:510
  116.9 3.5 %all-to-all-start.2 = ((f32[4,128,256]{2,1,0:T(8,128)}), f32[4,128,256]{2,1,0:T(8,128)S(1)}, u32[]{:S(2)}, u32[]{:S(2)}) async-start(f32[4,128,256]{2,1,0:T(8,128)} %bitcast.16), calls=%async_computation.2 | async-start | bytes 1048576 | tf_op jit(solution)/shard_map/all_to_all | solution.py:519
  120.4 0.8 copy.15
  121.1 0.8 copy.16
  121.9 8.5 %all-to-all-done.2 = f32[4,128,256]{2,1,0:T(8,128)S(1)} async-done(((f32[4,128,256]{2,1,0:T(8,128)}), f32[4,128,256]{2,1,0:T(8,128)S(1)}, u32[]{:S(2)}, u32[]{:S(2)}) %all-to-all-start.2) | async-done | bytes 524320 | tf_op jit(solution)/shard_map/all_to_all | solution.py:519
  130.4 0.7 slice_add_fusion
Async XLA Ops:
  0.6 68.5 %copy-start.2 = (bf16[128,128]{1,0:T(8,128)(2,1)S(1)}, bf16[128,128]{1,0:T(8,128)(2,1)}, u32[]{:S(2)}) copy-start(bf16[128,128]{1,0:T(8,128)(2,1)} %constant.6.clone.band_ref) | copy-start | bytes 98308
  4.3 64.8 %copy-start.1 = (f32[2048,128]{1,0:T(8,128)S(1)}, f32[2048,128]{1,0:T(8,128)}, u32[]{:S(2)}) copy-start(f32[2048,128]{1,0:T(8,128)} %get-tuple-element.14) | copy-start | bytes 3145732
  4.4 27.5 %collective-permute-start.4 = (f32[2048,128]{1,0:T(8,128)}, f32[2048,128]{1,0:T(8,128)S(1)}, u32[]{:S(2)}, u32[]{:S(2)}) collective-permute-start(f32[2048,128]{1,0:T(8,128)} %get-tuple-element.14), channel_id=1, source_target_pairs={{0,3},{1,0},{2,1},{3,2},{4,7},{5,4},{6,5},{7,6},{8,11},{9,8},{10,9... | collective-permute-start | bytes 3145736 | tf_op jit(solution)/shard_map/ppermute | solution.py:392
  9.2 29.0 %collective-permute-start.3 = (f32[2048,128]{1,0:T(8,128)}, f32[2048,128]{1,0:T(8,128)S(1)}, u32[]{:S(2)}, u32[]{:S(2)}) collective-permute-start(f32[2048,128]{1,0:T(8,128)} %get-tuple-element.14), channel_id=1, source_target_pairs={{0,1},{1,2},{2,3},{3,0},{4,5},{5,6},{6,7},{7,4},{8,9},{9,10},{10,1... | collective-permute-start | bytes 3145736 | tf_op jit(solution)/shard_map/ppermute | solution.py:392
  11.1 41.2 %all-to-all-start = ((f32[128,4,128]{2,1,0:T(4,128)}), f32[128,4,128]{2,1,0:T(4,128)S(1)}, u32[]{:S(2)}, u32[]{:S(2)}) async-start(f32[128,4,128]{2,1,0:T(4,128)} %bitcast.35), calls=%async_computation | async-start | bytes 524288 | tf_op jit(solution)/shard_map/all_to_all | solution.py:458
  32.7 36.4 %collective-permute-start.6 = (f32[1024,128]{1,0:T(8,128)}, f32[1024,128]{1,0:T(8,128)}, u32[]{:S(2)}, u32[]{:S(2)}) collective-permute-start(f32[1024,128]{1,0:T(8,128)} %slice.25), channel_id=1, source_target_pairs={{0,3},{1,0},{2,1},{3,2},{4,7},{5,4},{6,5},{7,6},{8,11},{9,8},{10,9... | collective-permute-start | bytes 1572872 | tf_op jit(solution)/shard_map/ppermute | solution.py:392
  39.0 30.1 %collective-permute-start.5 = (f32[1024,128]{1,0:T(8,128)}, f32[1024,128]{1,0:T(8,128)}, u32[]{:S(2)}, u32[]{:S(2)}) collective-permute-start(f32[1024,128]{1,0:T(8,128)} %slice.24), channel_id=1, source_target_pairs={{0,1},{1,2},{2,3},{3,0},{4,5},{5,6},{6,7},{7,4},{8,9},{9,10},{10,1... | collective-permute-start | bytes 1572872 | tf_op jit(solution)/shard_map/ppermute | solution.py:392
  52.3 19.3 %collective-permute-start.2 = (f32[512,128]{1,0:T(8,128)S(1)}, f32[512,128]{1,0:T(8,128)}, u32[]{:S(2)}, u32[]{:S(2)}) collective-permute-start(f32[512,128]{1,0:T(8,128)S(1)} %bitcast.26), channel_id=1, source_target_pairs={{0,2},{1,3},{2,0},{3,1},{4,6},{5,7},{6,4},{7,5},{8,10},{9,11},{10,... | collective-permute-start | bytes 786440 | tf_op jit(solution)/shard_map/ppermute | solution.py:392
  56.5 15.2 %collective-permute-start.1 = (f32[512,128]{1,0:T(8,128)S(1)}, f32[512,128]{1,0:T(8,128)}, u32[]{:S(2)}, u32[]{:S(2)}) collective-permute-start(f32[512,128]{1,0:T(8,128)S(1)} %bitcast.27), channel_id=1, source_target_pairs={{0,3},{1,0},{2,1},{3,2},{4,7},{5,4},{6,5},{7,6},{8,11},{9,8},{10,9... | collective-permute-start | bytes 786440 | tf_op jit(solution)/shard_map/ppermute | solution.py:392
  59.5 12.1 %collective-permute-start = (f32[512,128]{1,0:T(8,128)S(1)}, f32[512,128]{1,0:T(8,128)}, u32[]{:S(2)}, u32[]{:S(2)}) collective-permute-start(f32[512,128]{1,0:T(8,128)S(1)} %bitcast.28), channel_id=1, source_target_pairs={{0,1},{1,2},{2,3},{3,0},{4,5},{5,6},{6,7},{7,4},{8,9},{9,10},{10,1... | collective-permute-start | bytes 786440 | tf_op jit(solution)/shard_map/ppermute | solution.py:392
  63.0 8.7 %copy-start.5 = (f32[1,3]{1,0:T(1,128)S(1)}, f32[1,3]{1,0:T(1,128)}, u32[]{:S(2)}) copy-start(f32[1,3]{1,0:T(1,128)} %wave_ref.1) | copy-start | bytes 40
  69.1 2.6 %copy-start = (f32[8192,128]{1,0:T(8,128)S(1)}, f32[8192,128]{1,0:T(8,128)}, u32[]{:S(2)}) copy-start(f32[8192,128]{1,0:T(8,128)} %receivers.1.extra_hbm) | copy-start | bytes 12582916
  71.7 42.2 %copy-start.3 = (s32[128]{0:T(128)S(1)}, s32[128]{0:T(128)}, u32[]{:S(2)}) copy-start(s32[128]{0:T(128)} %ax_ref.1) | copy-start | bytes 1540
  71.7 42.2 %copy-start.4 = (s32[128]{0:T(128)S(1)}, s32[128]{0:T(128)}, u32[]{:S(2)}) copy-start(s32[128]{0:T(128)} %ay_ref.1) | copy-start | bytes 1540
  116.9 13.5 %all-to-all-start.2 = ((f32[4,128,256]{2,1,0:T(8,128)}), f32[4,128,256]{2,1,0:T(8,128)S(1)}, u32[]{:S(2)}, u32[]{:S(2)}) async-start(f32[4,128,256]{2,1,0:T(8,128)} %bitcast.16), calls=%async_computation.2 | async-start | bytes 1048576 | tf_op jit(solution)/shard_map/all_to_all | solution.py:519

commit v4 on v3

--- a/solution.py
+++ b/solution.py
@@ -72,25 +72,28 @@
     lax.fori_loop(0, depth // ROWS, body, 0, unroll=8)
 
 
-def spread_kernel(shots, width_x, me_ref, ax_ref, ay_ref, in_ref, out_ref, near_ref, far_ref):
+def spread_kernel(shots, width_x, me_ref, ax_ref, ay_ref, in_ref, out_ref, *sum_refs):
     width_y = in_ref.shape[1]
     first = me_ref[0] * width_x
-    near_ref[...] = jnp.zeros_like(near_ref)
-    far_ref[...] = jnp.zeros_like(far_ref)
+    for ref in sum_refs:
+        ref[...] = jnp.zeros_like(ref)
     lane = lax.broadcasted_iota(jnp.int32, (width_x, width_y), 1)
-
-    def body(shot, carry):
-        start = pl.multiple_of(shot * width_x, width_x)
-        column = ay_ref[shot]
-        moved = pltpu.roll(in_ref[pl.ds(start, width_x), :], lax.rem(column, width_y), 1)
-        rows = pl.ds(ax_ref[shot] + first, width_x)
-        near_ref[rows, :] = near_ref[rows, :] + jnp.where(lane < column, 0.0, moved)
-        far_ref[rows, :] = far_ref[rows, :] + jnp.where(lane < column, moved, 0.0)
+    pairs = [sum_refs[index : index + 2] for index in range(0, len(sum_refs), 2)]
+
+    def body(group, carry):
+        for member, (near_ref, far_ref) in enumerate(pairs):
+            shot = group * len(pairs) + member
+            start = pl.multiple_of(shot * width_x, width_x)
+            column = ay_ref[shot]
+            moved = pltpu.roll(in_ref[pl.ds(start, width_x), :], lax.rem(column, width_y), 1)
+            rows = pl.ds(ax_ref[shot] + first, width_x)
+            near_ref[rows, :] = near_ref[rows, :] + jnp.where(lane < column, 0.0, moved)
+            far_ref[rows, :] = far_ref[rows, :] + jnp.where(lane < column, moved, 0.0)
         return carry
 
-    lax.fori_loop(0, shots, body, 0, unroll=8)
-    out_ref[:, :width_y] = near_ref[...]
-    out_ref[:, width_y:] = far_ref[...]
+    lax.fori_loop(0, shots // len(pairs), body, 0, unroll=16)
+    out_ref[:, :width_y] = sum(ref[...] for ref, _ in pairs)
+    out_ref[:, width_y:] = sum(ref[...] for _, ref in pairs)
 
 
 def cell(flat, across, width_y):
@@ -131,7 +134,7 @@
             out_ref[pl.ds(start, 4), :] = total
         return carry
 
-    lax.fori_loop(0, count // GROUP, body, 0, unroll=4)
+    lax.fori_loop(0, count // GROUP, body, 0, unroll=16)
 
 
 def first_kernel(
@@ -186,7 +189,7 @@
         panels_ref[pl.ds(start, width_x), :] = jnp.where(lane < width_y - column, near, far)
         return carry
 
-    lax.fori_loop(0, shots, cut, 0, unroll=8)
+    lax.fori_loop(0, shots, cut, 0, unroll=128)
     keep_panels = pltpu.make_async_copy(panels_ref, panels_hbm, out_sems.at[1])
     keep_panels.start()
     keep_fields.wait()
@@ -305,14 +308,16 @@
 
         over_rows(depth, step)
 
-    by_slabs(step_one, across)
+    for slab in range(slabs):
+        step_one(slab * width_x)
     add_source(one_ref, 0)
 
     def step_two(x):
-        along(one_ref, x, width_x, band_ref, part_ref)
+        part = part_ref if x // width_x % 2 else other_ref
+        along(one_ref, x, width_x, band_ref, part)
 
         def step(rows, _):
-            for index, bend in enumerate(laplace(one_ref, x, width_x, rows, part_ref)):
+            for index, bend in enumerate(laplace(one_ref, x, width_x, rows, part)):
                 here = x + index
                 curve_one_ref[here, rows, :] = bend
                 two_ref[here + REACH, rows, :] = (
@@ -323,7 +328,8 @@
 
         over_rows(depth, step)
 
-    by_slabs(step_two, across)
+    for slab in range(slabs):
+        step_two(slab * width_x)
     add_source(two_ref, 1)
 
     def back_three(x):
@@ -471,9 +477,10 @@
         name="before",
     )(me, *(piece.reshape(-1, depth, width_y) for piece in (fields, left, right, far_a, far_b)), weights)
 
+    speed, extra = lax.optimization_barrier((speed, extra))
+    speed_left = shift(speed, 1)
+    speed_right = shift(speed, -1)
     speed_far = shift(speed, 2)
-    speed_right = shift(speed, -1)
-    speed_left = shift(speed, 1)
 
     slab = jax.ShapeDtypeStruct((width_x, depth, width_y), jnp.bfloat16)
     grad, first, second = pl.pallas_call(
@@ -512,7 +519,7 @@
         out_shape=shape(model_x, model_y),
         in_specs=[SMEM, SMEM, SMEM, VMEM],
         out_specs=VMEM,
-        scratch_shapes=[pltpu.VMEM((model_x, width_y), f32)] * 2,
+        scratch_shapes=[pltpu.VMEM((model_x, width_y), f32)] * 8,
         compiler_params=PARAMS,
         name="spread",
     )(me, anchor_x, anchor_y, returned)

time: 132 us -> 129 us (0.977)
  Pallas kernels: 21.9 us -> 18.9 us
    all_to_all x1, waiting for transfers between devices: 11.3 us -> 5.46 us  [per_device(): lax.all_to_all(panels.reshape(groups, width_x, width_y), 'shots', split_a...]
    ppermute x7, waiting for transfers between devices: 1.5 us -> 6.63 us  [shift(): lax.ppermute(x, 'sub', [(i, (i + distance) % count) for i in range(count)])]
  transfers between devices with their start and end apart: 9 -> 9, of which waited for: 3 -> 5; matrix products, arithmetic and copies ran while one was open for 2% -> 2% of each run, Pallas kernels for 7% -> 6%
where the time goes in v4:
time: 129 us; the launch traced here: 128 us
  starting transfers between devices  47.2 us (37%)
  blocking collectives  36.3 us (28%)
  waiting for transfers between devices  20.6 us (16%)
  Pallas kernels  18.9 us (15%)
  local copies, waits for them, and re-layouts  3.21 us (2%)
  between operations  1.47 us (1%)
    all_to_all x1, blocking collectives, per_device(): lax.all_to_all(grad.reshape(groups, width_x, width_y), 'shots', split_axi...  36.3 us
    ppermute x7, starting transfers between devices, shift(): lax.ppermute(x, 'sub', [(i, (i + distance) % count) for i in range(count)])  24.4 us
    all_to_all x1, starting transfers between devices, per_device(): lax.all_to_all(panels.reshape(groups, width_x, width_y), 'shots', split_a...  19.3 us
    all_to_all x1, waiting for transfers between devices, per_device(): lax.all_to_all(owned.reshape(slabs, model_x // slabs, model_y), 'sub', sp...  8.48 us
    ppermute x7, waiting for transfers between devices, shift(): lax.ppermute(x, 'sub', [(i, (i + distance) % count) for i in range(count)])  6.63 us
    pallas_call x1, Pallas kernels, per_device(): pl.pallas_call(functools.partial(receiver_kernel, rec_index.shape[1], acr...  5.87 us
    pallas_call x1, Pallas kernels, per_device(): pl.pallas_call(functools.partial(main_kernel, slabs, depth, width_x), out...  5.67 us
    all_to_all x1, waiting for transfers between devices, per_device(): lax.all_to_all(panels.reshape(groups, width_x, width_y), 'shots', split_a...  5.46 us
  transfers between devices with their start and end apart: 9, of which 5 were waited for; matrix products, arithmetic and copies ran while one was open for 2% of the time, Pallas kernels for 6%

profile of v4, /device:TPU:24, one launch (start us, length us, event | category | flops | bytes accessed | tf_op | source)
XLA Modules:
  0.0 128.2 jit_solution(2531674236174447653)
XLA Ops:
  0.6 0.0 copy-start.2
  0.6 2.8 %first.1 = (f32[2048,128]{1,0:T(8,128)}, f32[512,128]{1,0:T(8,128)}) custom-call(s32[1]{0:T(128)} %bitcast.me_ref, s32[128]{0:T(128)} %ax_ref.1, s32[128]{0:T(128)} %ay_ref.1, f32[512,256]{1,0:T(8,128)} %bitcast.34, bf16[128,4,128]{2,1,0:T(4,128)(2,1)} %bitcast.36, bf16[128,4,128]{2,1,0:T(4,128)(2,1)} %bitcast.37, bf16[128,4,128]{2,1,0:T(4,128)(2,1)} %bitcast.38, ...), custom_call_target="tpu_custom_call" | custom-call | tf_op jit(solution)/shard_map/first/pallas_call | solution.py:428
  3.5 0.0 copy-start.1
  3.5 4.8 %collective-permute-start.4 = (f32[2048,128]{1,0:T(8,128)}, f32[2048,128]{1,0:T(8,128)S(1)}, u32[]{:S(2)}, u32[]{:S(2)}) collective-permute-start(f32[2048,128]{1,0:T(8,128)} %get-tuple-element.17), channel_id=1, source_target_pairs={{0,3},{1,0},{2,1},{3,2},{4,7},{5,4},{6,5},{7,6},{8,11},{9,8},{10,9... | collective-permute-start | bytes 3145736 | tf_op jit(solution)/shard_map/ppermute | solution.py:398
  8.3 1.9 %collective-permute-start.3 = (f32[2048,128]{1,0:T(8,128)}, f32[2048,128]{1,0:T(8,128)S(1)}, u32[]{:S(2)}, u32[]{:S(2)}) collective-permute-start(f32[2048,128]{1,0:T(8,128)} %get-tuple-element.17), channel_id=1, source_target_pairs={{0,1},{1,2},{2,3},{3,0},{4,5},{5,6},{6,7},{7,4},{8,9},{9,10},{10,1... | collective-permute-start | bytes 3145736 | tf_op jit(solution)/shard_map/ppermute | solution.py:398
  10.2 19.3 %all-to-all-start = ((f32[128,4,128]{2,1,0:T(4,128)}), f32[128,4,128]{2,1,0:T(4,128)S(1)}, u32[]{:S(2)}, u32[]{:S(2)}) async-start(f32[128,4,128]{2,1,0:T(4,128)} %bitcast.35), calls=%async_computation | async-start | bytes 524288 | tf_op jit(solution)/shard_map/all_to_all | solution.py:464
  29.5 1.5 %collective-permute-done.4 = f32[2048,128]{1,0:T(8,128)S(1)} collective-permute-done((f32[2048,128]{1,0:T(8,128)}, f32[2048,128]{1,0:T(8,128)S(1)}, u32[]{:S(2)}, u32[]{:S(2)}) %collective-permute-start.4) | collective-permute-done | bytes 1048608 | tf_op jit(solution)/shard_map/ppermute | solution.py:398
  31.0 0.8 slice.25
  31.8 5.5 %collective-permute-start.6 = (f32[1024,128]{1,0:T(8,128)}, f32[1024,128]{1,0:T(8,128)}, u32[]{:S(2)}, u32[]{:S(2)}) collective-permute-start(f32[1024,128]{1,0:T(8,128)} %slice.25), channel_id=1, source_target_pairs={{0,3},{1,0},{2,1},{3,2},{4,7},{5,4},{6,5},{7,6},{8,11},{9,8},{10,9... | collective-permute-start | bytes 1572872 | tf_op jit(solution)/shard_map/ppermute | solution.py:398
  37.3 0.0 collective-permute-done.3
  37.3 0.8 slice.24
  38.1 1.9 %collective-permute-start.5 = (f32[1024,128]{1,0:T(8,128)}, f32[1024,128]{1,0:T(8,128)}, u32[]{:S(2)}, u32[]{:S(2)}) collective-permute-start(f32[1024,128]{1,0:T(8,128)} %slice.24), channel_id=1, source_target_pairs={{0,1},{1,2},{2,3},{3,0},{4,5},{5,6},{6,7},{7,4},{8,9},{9,10},{10,1... | collective-permute-start | bytes 1572872 | tf_op jit(solution)/shard_map/ppermute | solution.py:398
  40.1 0.0 copy-start.5
  40.1 5.9 %receivers.1.extra_hbm = f32[8192,128]{1,0:T(8,128)} custom-call(s32[1,512]{1,0:T(1,128)} %index_hbm.1, f32[3,1,512]{2,1,0:T(1,128)} %bitcast.40), custom_call_target="tpu_custom_call" | custom-call | tf_op jit(solution)/shard_map/receivers/pallas_call | solution.py:448
  45.9 5.5 %all-to-all-done = f32[128,4,128]{2,1,0:T(4,128)S(1)} async-done(((f32[128,4,128]{2,1,0:T(4,128)}), f32[128,4,128]{2,1,0:T(4,128)S(1)}, u32[]{:S(2)}, u32[]{:S(2)}) %all-to-all-start) | async-done | bytes 262176 | tf_op jit(solution)/shard_map/all_to_all | solution.py:464
  51.4 0.0 copy-start
  51.4 4.4 %collective-permute-start.2 = (f32[512,128]{1,0:T(8,128)S(1)}, f32[512,128]{1,0:T(8,128)S(1)}, u32[]{:S(2)}, u32[]{:S(2)}) collective-permute-start(f32[512,128]{1,0:T(8,128)S(1)} %bitcast.26), channel_id=1, source_target_pairs={{0,2},{1,3},{2,0},{3,1},{4,6},{5,7},{6,4},{7,5},{8,10},{9,11},{10,... | collective-permute-start | bytes 786440 | tf_op jit(solution)/shard_map/ppermute | solution.py:398
  55.9 3.0 %collective-permute-start.1 = (f32[512,128]{1,0:T(8,128)S(1)}, f32[512,128]{1,0:T(8,128)S(1)}, u32[]{:S(2)}, u32[]{:S(2)}) collective-permute-start(f32[512,128]{1,0:T(8,128)S(1)} %bitcast.27), channel_id=1, source_target_pairs={{0,3},{1,0},{2,1},{3,2},{4,7},{5,4},{6,5},{7,6},{8,11},{9,8},{10,9... | collective-permute-start | bytes 786440 | tf_op jit(solution)/shard_map/ppermute | solution.py:398
  58.9 2.8 %collective-permute-start = (f32[512,128]{1,0:T(8,128)S(1)}, f32[512,128]{1,0:T(8,128)S(1)}, u32[]{:S(2)}, u32[]{:S(2)}) collective-permute-start(f32[512,128]{1,0:T(8,128)S(1)} %bitcast.28), channel_id=1, source_target_pairs={{0,1},{1,2},{2,3},{3,0},{4,5},{5,6},{6,7},{7,4},{8,9},{9,10},{10,1... | collective-permute-start | bytes 786440 | tf_op jit(solution)/shard_map/ppermute | solution.py:398
  62.4 0.0 collective-permute-done.6
  62.4 0.0 collective-permute-done.5
  62.4 0.0 copy-done.2
  62.4 0.0 copy-done.1
  62.4 2.3 %before.1 = (f32[24,128,128]{2,1,0:T(8,128)S(1)}, f32[16,128,128]{2,1,0:T(8,128)S(1)}, f32[16,128,128]{2,1,0:T(8,128)S(1)}, f32[16,128,128]{2,1,0:T(8,128)S(1)}, f32[16,128,128]{2,1,0:T(8,128)S(1)}) custom-call(s32[1]{0:T(128)} %bitcast.me_ref, f32[16,128,128]{2,1,0:T(8,128)S(1)} %bitcast.25, f32[16,128,128]{2,1,0:T(8,128)S(1)} %bitcast.24, ...), custom_call_target="tpu_custom_call" | custom-call | tf_op jit(solution)/shard_map/before/pallas_call | solution.py:470
  64.7 0.0 collective-permute-done.2.far_ref
  64.7 4.9 %collective-permute-done.1.right_ref = f32[512,128]{1,0:T(8,128)S(1)} collective-permute-done((f32[512,128]{1,0:T(8,128)S(1)}, f32[512,128]{1,0:T(8,128)S(1)}, u32[]{:S(2)}, u32[]{:S(2)}) %collective-permute-start.1) | collective-permute-done | bytes 262176 | tf_op jit(solution)/shard_map/ppermute | solution.py:398
  69.6 0.3 collective-permute-done.left_ref
  69.9 0.0 copy-done.5
  69.9 0.0 copy-done
  69.9 0.0 copy-start.3
  69.9 0.0 copy-start.4
  69.9 5.7 %window.1 = (f32[512,128]{1,0:T(8,128)S(1)}, bf16[4,128,128]{2,1,0:T(8,128)(2,1)S(1)}, bf16[4,128,128]{2,1,0:T(8,128)(2,1)S(1)}) custom-call(s32[1]{0:T(128)} %bitcast.me_ref, s32[1]{0:T(128)S(6)} %copy.17.source_ref, f32[1,3]{1,0:T(1,128)S(1)} %copy-done.5, f32[512,128]{1,0:T(8,128)S(1)} %bitcast.29, f32[512,128]{1,0:T(8,128)S(1)} %collective-permute-done.left_ref, ...), custom_call_target="tpu_custom_call" | custom-call | tf_op jit(solution)/shard_map/window/pallas_call | solution.py:486
  75.6 36.3 %all_to_all.15 = f32[128,4,128]{2,1,0:T(4,128)S(1)} all-to-all(f32[128,4,128]{2,1,0:T(4,128)S(1)} %bitcast.31), channel_id=1, replica_groups=mesh['shots'=128,'sub'=4] {'shots'}, dimensions={0} | all-to-all | bytes 524288 | tf_op jit(solution)/shard_map/all_to_all | solution.py:514
  111.9 0.0 copy-done.3
  111.9 0.0 copy-done.4
  111.9 2.2 %spread.1 = f32[512,256]{1,0:T(8,128)} custom-call(s32[1]{0:T(128)} %bitcast.me_ref, s32[128]{0:T(128)S(1)} %copy-done.3, s32[128]{0:T(128)S(1)} %copy-done.4, f32[512,128]{1,0:T(8,128)S(1)} %bitcast.30), custom_call_target="tpu_custom_call" | custom-call | tf_op jit(solution)/shard_map/spread/pallas_call | solution.py:517
  114.1 3.5 %all-to-all-start.2 = ((f32[4,128,256]{2,1,0:T(8,128)}), f32[4,128,256]{2,1,0:T(8,128)S(1)}, u32[]{:S(2)}, u32[]{:S(2)}) async-start(f32[4,128,256]{2,1,0:T(8,128)} %bitcast.16), calls=%async_computation.2 | async-start | bytes 1048576 | tf_op jit(solution)/shard_map/all_to_all | solution.py:526
  117.6 0.8 copy.15
  118.3 0.8 copy.16
  119.1 8.5 %all-to-all-done.2 = f32[4,128,256]{2,1,0:T(8,128)S(1)} async-done(((f32[4,128,256]{2,1,0:T(8,128)}), f32[4,128,256]{2,1,0:T(8,128)S(1)}, u32[]{:S(2)}, u32[]{:S(2)}) %all-to-all-start.2) | async-done | bytes 524320 | tf_op jit(solution)/shard_map/all_to_all | solution.py:526
  127.6 0.7 slice_add_fusion
Async XLA Ops:
  0.6 61.8 %copy-start.2 = (bf16[128,128]{1,0:T(8,128)(2,1)S(1)}, bf16[128,128]{1,0:T(8,128)(2,1)}, u32[]{:S(2)}) copy-start(bf16[128,128]{1,0:T(8,128)(2,1)} %constant.6.clone.band_ref) | copy-start | bytes 98308
  3.5 58.9 %copy-start.1 = (f32[2048,128]{1,0:T(8,128)S(1)}, f32[2048,128]{1,0:T(8,128)}, u32[]{:S(2)}) copy-start(f32[2048,128]{1,0:T(8,128)} %get-tuple-element.17) | copy-start | bytes 3145732
  3.5 27.5 %collective-permute-start.4 = (f32[2048,128]{1,0:T(8,128)}, f32[2048,128]{1,0:T(8,128)S(1)}, u32[]{:S(2)}, u32[]{:S(2)}) collective-permute-start(f32[2048,128]{1,0:T(8,128)} %get-tuple-element.17), channel_id=1, source_target_pairs={{0,3},{1,0},{2,1},{3,2},{4,7},{5,4},{6,5},{7,6},{8,11},{9,8},{10,9... | collective-permute-start | bytes 3145736 | tf_op jit(solution)/shard_map/ppermute | solution.py:398
  8.3 29.0 %collective-permute-start.3 = (f32[2048,128]{1,0:T(8,128)}, f32[2048,128]{1,0:T(8,128)S(1)}, u32[]{:S(2)}, u32[]{:S(2)}) collective-permute-start(f32[2048,128]{1,0:T(8,128)} %get-tuple-element.17), channel_id=1, source_target_pairs={{0,1},{1,2},{2,3},{3,0},{4,5},{5,6},{6,7},{7,4},{8,9},{9,10},{10,1... | collective-permute-start | bytes 3145736 | tf_op jit(solution)/shard_map/ppermute | solution.py:398
  10.2 41.2 %all-to-all-start = ((f32[128,4,128]{2,1,0:T(4,128)}), f32[128,4,128]{2,1,0:T(4,128)S(1)}, u32[]{:S(2)}, u32[]{:S(2)}) async-start(f32[128,4,128]{2,1,0:T(4,128)} %bitcast.35), calls=%async_computation | async-start | bytes 524288 | tf_op jit(solution)/shard_map/all_to_all | solution.py:464
  31.8 30.5 %collective-permute-start.6 = (f32[1024,128]{1,0:T(8,128)}, f32[1024,128]{1,0:T(8,128)}, u32[]{:S(2)}, u32[]{:S(2)}) collective-permute-start(f32[1024,128]{1,0:T(8,128)} %slice.25), channel_id=1, source_target_pairs={{0,3},{1,0},{2,1},{3,2},{4,7},{5,4},{6,5},{7,6},{8,11},{9,8},{10,9... | collective-permute-start | bytes 1572872 | tf_op jit(solution)/shard_map/ppermute | solution.py:398
  38.1 24.2 %collective-permute-start.5 = (f32[1024,128]{1,0:T(8,128)}, f32[1024,128]{1,0:T(8,128)}, u32[]{:S(2)}, u32[]{:S(2)}) collective-permute-start(f32[1024,128]{1,0:T(8,128)} %slice.24), channel_id=1, source_target_pairs={{0,1},{1,2},{2,3},{3,0},{4,5},{5,6},{6,7},{7,4},{8,9},{9,10},{10,1... | collective-permute-start | bytes 1572872 | tf_op jit(solution)/shard_map/ppermute | solution.py:398
  40.1 29.8 %copy-start.5 = (f32[1,3]{1,0:T(1,128)S(1)}, f32[1,3]{1,0:T(1,128)}, u32[]{:S(2)}) copy-start(f32[1,3]{1,0:T(1,128)} %wave_ref.1) | copy-start | bytes 40
  51.4 18.5 %copy-start = (f32[8192,128]{1,0:T(8,128)S(1)}, f32[8192,128]{1,0:T(8,128)}, u32[]{:S(2)}) copy-start(f32[8192,128]{1,0:T(8,128)} %receivers.1.extra_hbm) | copy-start | bytes 12582916
  51.4 13.3 %collective-permute-start.2 = (f32[512,128]{1,0:T(8,128)S(1)}, f32[512,128]{1,0:T(8,128)S(1)}, u32[]{:S(2)}, u32[]{:S(2)}) collective-permute-start(f32[512,128]{1,0:T(8,128)S(1)} %bitcast.26), channel_id=1, source_target_pairs={{0,2},{1,3},{2,0},{3,1},{4,6},{5,7},{6,4},{7,5},{8,10},{9,11},{10,... | collective-permute-start | bytes 786440 | tf_op jit(solution)/shard_map/ppermute | solution.py:398
  55.9 13.7 %collective-permute-start.1 = (f32[512,128]{1,0:T(8,128)S(1)}, f32[512,128]{1,0:T(8,128)S(1)}, u32[]{:S(2)}, u32[]{:S(2)}) collective-permute-start(f32[512,128]{1,0:T(8,128)S(1)} %bitcast.27), channel_id=1, source_target_pairs={{0,3},{1,0},{2,1},{3,2},{4,7},{5,4},{6,5},{7,6},{8,11},{9,8},{10,9... | collective-permute-start | bytes 786440 | tf_op jit(solution)/shard_map/ppermute | solution.py:398
  58.9 11.0 %collective-permute-start = (f32[512,128]{1,0:T(8,128)S(1)}, f32[512,128]{1,0:T(8,128)S(1)}, u32[]{:S(2)}, u32[]{:S(2)}) collective-permute-start(f32[512,128]{1,0:T(8,128)S(1)} %bitcast.28), channel_id=1, source_target_pairs={{0,1},{1,2},{2,3},{3,0},{4,5},{5,6},{6,7},{7,4},{8,9},{9,10},{10,1... | collective-permute-start | bytes 786440 | tf_op jit(solution)/shard_map/ppermute | solution.py:398
  69.9 42.0 %copy-start.3 = (s32[128]{0:T(128)S(1)}, s32[128]{0:T(128)}, u32[]{:S(2)}) copy-start(s32[128]{0:T(128)} %ax_ref.1) | copy-start | bytes 1540
  69.9 42.0 %copy-start.4 = (s32[128]{0:T(128)S(1)}, s32[128]{0:T(128)}, u32[]{:S(2)}) copy-start(s32[128]{0:T(128)} %ay_ref.1) | copy-start | bytes 1540
  114.1 13.5 %all-to-all-start.2 = ((f32[4,128,256]{2,1,0:T(8,128)}), f32[4,128,256]{2,1,0:T(8,128)S(1)}, u32[]{:S(2)}, u32[]{:S(2)}) async-start(f32[4,128,256]{2,1,0:T(8,128)} %bitcast.16), calls=%async_computation.2 | async-start | bytes 1048576 | tf_op jit(solution)/shard_map/all_to_all | solution.py:526

commit v5 on v4

--- a/solution.py
+++ b/solution.py
@@ -137,24 +137,13 @@
     lax.fori_loop(0, count // GROUP, body, 0, unroll=16)
 
 
-def first_kernel(
-    shots, depth, width_x, me_ref, ax_hbm, ay_hbm, model_hbm, before_hbm, now_hbm, later_hbm, latest_hbm,
-    fields_hbm, panels_hbm,
-    near_ref, far_ref, before_ref, now_ref, later_ref, latest_ref, turn_ref, fields_ref, panels_ref, ax_ref, ay_ref, in_sems, out_sems,
+def fields_kernel(
+    depth, width_x, before_hbm, now_hbm, later_hbm, latest_hbm, out_ref, before_ref, now_ref, later_ref, latest_ref, turn_ref, sems
 ):
     block = depth * width_x
-    width_y = panels_ref.shape[1]
-    pairs = (
-        (now_hbm, now_ref),
-        (before_hbm, before_ref),
-        (later_hbm, later_ref),
-        (latest_hbm, latest_ref),
-        (model_hbm.at[:, :width_y], near_ref),
-        (model_hbm.at[:, width_y:], far_ref),
-        (ax_hbm, ax_ref),
-        (ay_hbm, ay_ref),
-    )
-    loads = [pltpu.make_async_copy(source, ref, in_sems.at[k]) for k, (source, ref) in enumerate(pairs)]
+    width_y = out_ref.shape[1]
+    pairs = ((now_hbm, now_ref), (before_hbm, before_ref), (later_hbm, later_ref), (latest_hbm, latest_ref))
+    loads = [pltpu.make_async_copy(source, ref, sems.at[k]) for k, (source, ref) in enumerate(pairs)]
     for load in loads:
         load.start()
 
@@ -162,9 +151,9 @@
         turn_ref[...] = value
         flat = turn_ref.reshape(block, width_y)
         for row in range(width_x):
-            fields_ref[pl.ds(place * block + row * depth, depth), :] = flat[pl.ds(row, depth, stride=width_x), :]
-
-    for load in loads[:4]:
+            out_ref[pl.ds(place * block + row * depth, depth), :] = flat[pl.ds(row, depth, stride=width_x), :]
+
+    for load in loads:
         load.wait()
     now = now_ref[...].astype(jnp.float32)
     put(0, now)
@@ -172,9 +161,20 @@
     later = later_ref[...].astype(jnp.float32)
     put(2, later)
     put(3, 2.0 * later - latest_ref[...].astype(jnp.float32))
-    keep_fields = pltpu.make_async_copy(fields_ref, fields_hbm, out_sems.at[0])
-    keep_fields.start()
-    for load in loads[4:]:
+
+
+def cut_kernel(shots, width_x, me_ref, ax_hbm, ay_hbm, model_hbm, out_ref, near_ref, far_ref, ax_ref, ay_ref, sems):
+    width_y = out_ref.shape[1]
+    pairs = (
+        (model_hbm.at[:, :width_y], near_ref),
+        (model_hbm.at[:, width_y:], far_ref),
+        (ax_hbm, ax_ref),
+        (ay_hbm, ay_ref),
+    )
+    loads = [pltpu.make_async_copy(source, ref, sems.at[k]) for k, (source, ref) in enumerate(pairs)]
+    for load in loads:
+        load.start()
+    for load in loads:
         load.wait()
     first = me_ref[0] * width_x
     lane = lax.broadcasted_iota(jnp.int32, (width_x, width_y), 1)
@@ -186,14 +186,10 @@
         near = pltpu.roll(near_ref[rows, :], turn, 1)
         far = pltpu.roll(far_ref[rows, :], turn, 1)
         start = pl.multiple_of(shot * width_x, width_x)
-        panels_ref[pl.ds(start, width_x), :] = jnp.where(lane < width_y - column, near, far)
+        out_ref[pl.ds(start, width_x), :] = jnp.where(lane < width_y - column, near, far)
         return carry
 
     lax.fori_loop(0, shots, cut, 0, unroll=128)
-    keep_panels = pltpu.make_async_copy(panels_ref, panels_hbm, out_sems.at[1])
-    keep_panels.start()
-    keep_fields.wait()
-    keep_panels.wait()
 
 
 def slab_slice(ref, first, depth, width_x, row):
@@ -425,24 +421,25 @@
         return jax.ShapeDtypeStruct(dims, f32)
 
     state = pltpu.VMEM((depth, width_x, width_y), jnp.bfloat16)
-    fields, panels = pl.pallas_call(
-        functools.partial(first_kernel, groups, depth, width_x),
-        out_shape=[shape(4 * block, width_y), shape(groups * width_x, width_y)],
-        in_specs=[SMEM] + [HBM] * 7,
-        out_specs=[HBM] * 2,
+    fields = pl.pallas_call(
+        functools.partial(fields_kernel, depth, width_x),
+        out_shape=shape(4 * block, width_y),
+        in_specs=[HBM] * 4,
+        out_specs=VMEM,
+        scratch_shapes=[state] * 4
+        + [pltpu.VMEM((depth, width_x, width_y), f32), pltpu.SemaphoreType.DMA((4,))],
+        name="fields",
+    )(state_before[0], state_now[0], adjoint_later[0], adjoint_latest[0])
+    panels = pl.pallas_call(
+        functools.partial(cut_kernel, groups, width_x),
+        out_shape=shape(groups * width_x, width_y),
+        in_specs=[SMEM] + [HBM] * 3,
+        out_specs=VMEM,
         scratch_shapes=[pltpu.VMEM((model_x, width_y), f32)] * 2
-        + [state] * 4
-        + [
-            pltpu.VMEM((depth, width_x, width_y), f32),
-            pltpu.VMEM((4 * block, width_y), f32),
-            pltpu.VMEM((groups * width_x, width_y), f32),
-            pltpu.SMEM((groups,), jnp.int32),
-            pltpu.SMEM((groups,), jnp.int32),
-            pltpu.SemaphoreType.DMA((8,)),
-            pltpu.SemaphoreType.DMA((2,)),
-        ],
-        name="first",
-    )(me, anchor_x, anchor_y, model[0], state_before[0], state_now[0], adjoint_later[0], adjoint_latest[0])
+        + [pltpu.SMEM((groups,), jnp.int32)] * 2
+        + [pltpu.SemaphoreType.DMA((4,))],
+        name="cut",
+    )(me, anchor_x, anchor_y, model[0])
     left = shift(fields, 1)
     right = shift(fields, -1)
     extra = pl.pallas_call(

time: 129 us -> 129 us (level)
  blocking collectives: 36.3 us -> 34 us
  Pallas kernels: 18.9 us -> 20.8 us
    all_to_all x1, blocking collectives: 36.3 us -> 34 us  [per_device(): lax.all_to_all(grad.reshape(groups, width_x, width_y), 'shots', split_axi...]
    pallas_call x1 -> x2, Pallas kernels: 2.8 us -> 4.78 us  [the longest x1 2.45 us: per_device(): pl.pallas_call(functools.partial(fields_kernel, depth, width_x), out_shap...]
    all_to_all x1, waiting for transfers between devices: 5.46 us -> 7.29 us  [per_device(): lax.all_to_all(panels.reshape(groups, width_x, width_y), 'shots', split_a...]
    ppermute x7, waiting for transfers between devices: 6.63 us -> 5.15 us  [shift(): lax.ppermute(x, 'sub', [(i, (i + distance) % count) for i in range(count)])]
  transfers between devices with their start and end apart: 9 -> 9, of which waited for: 5 -> 4; matrix products, arithmetic and copies ran while one was open for 2% -> 2% of each run, Pallas kernels for 6% -> 8%
where the time goes in v5:
time: 129 us; the launch traced here: 128 us
  starting transfers between devices  46.8 us (36%)
  blocking collectives  34 us (26%)
  waiting for transfers between devices  20.9 us (16%)
  Pallas kernels  20.8 us (16%)
  local copies, waits for them, and re-layouts  3.2 us (2%)
  between operations  1.49 us (1%)
    all_to_all x1, blocking collectives, per_device(): lax.all_to_all(grad.reshape(groups, width_x, width_y), 'shots', split_axi...  34 us
    ppermute x7, starting transfers between devices, shift(): lax.ppermute(x, 'sub', [(i, (i + distance) % count) for i in range(count)])  24 us
    all_to_all x1, starting transfers between devices, per_device(): lax.all_to_all(panels.reshape(groups, width_x, width_y), 'shots', split_a...  19.3 us
    all_to_all x1, waiting for transfers between devices, per_device(): lax.all_to_all(owned.reshape(slabs, model_x // slabs, model_y), 'sub', sp...  8.48 us
    all_to_all x1, waiting for transfers between devices, per_device(): lax.all_to_all(panels.reshape(groups, width_x, width_y), 'shots', split_a...  7.29 us
    pallas_call x1, Pallas kernels, per_device(): pl.pallas_call(functools.partial(receiver_kernel, rec_index.shape[1], acr...  5.87 us
    pallas_call x1, Pallas kernels, per_device(): pl.pallas_call(functools.partial(main_kernel, slabs, depth, width_x), out...  5.67 us
    ppermute x7, waiting for transfers between devices, shift(): lax.ppermute(x, 'sub', [(i, (i + distance) % count) for i in range(count)])  5.15 us
  transfers between devices with their start and end apart: 9, of which 4 were waited for; matrix products, arithmetic and copies ran while one was open for 2% of the time, Pallas kernels for 8%

profile of v5, /device:TPU:24, one launch (start us, length us, event | category | flops | bytes accessed | tf_op | source)
XLA Modules:
  0.0 127.9 jit_solution(626322871987769500)
XLA Ops:
  0.6 2.4 %fields.1 = f32[2048,128]{1,0:T(8,128)} custom-call(bf16[128,4,128]{2,1,0:T(4,128)(2,1)} %bitcast.36, bf16[128,4,128]{2,1,0:T(4,128)(2,1)} %bitcast.37, bf16[128,4,128]{2,1,0:T(4,128)(2,1)} %bitcast.38, bf16[128,4,128]{2,1,0:T(4,128)(2,1)} %bitcast.39), custom_call_target="tpu_custom_call" | custom-call | tf_op jit(solution)/shard_map/fields/pallas_call | solution.py:424
  3.1 0.0 copy-start.1
  3.1 0.0 copy-start.2
  3.1 4.8 %collective-permute-start.4 = (f32[2048,128]{1,0:T(8,128)}, f32[2048,128]{1,0:T(8,128)S(1)}, u32[]{:S(2)}, u32[]{:S(2)}) collective-permute-start(f32[2048,128]{1,0:T(8,128)} %fields.1), channel_id=1, source_target_pairs={{0,3},{1,0},{2,1},{3,2},{4,7},{5,4},{6,5},{7,6},{8,11},{9,8},{10,9... | collective-permute-start | bytes 3145736 | tf_op jit(solution)/shard_map/ppermute | solution.py:394
  7.9 1.9 %collective-permute-start.3 = (f32[2048,128]{1,0:T(8,128)}, f32[2048,128]{1,0:T(8,128)S(1)}, u32[]{:S(2)}, u32[]{:S(2)}) collective-permute-start(f32[2048,128]{1,0:T(8,128)} %fields.1), channel_id=1, source_target_pairs={{0,1},{1,2},{2,3},{3,0},{4,5},{5,6},{6,7},{7,4},{8,9},{9,10},{10,1... | collective-permute-start | bytes 3145736 | tf_op jit(solution)/shard_map/ppermute | solution.py:394
  9.8 2.3 %cut.1 = f32[512,128]{1,0:T(8,128)} custom-call(s32[1]{0:T(128)} %bitcast.me_ref, s32[128]{0:T(128)} %ax_ref.1, s32[128]{0:T(128)} %ay_ref.1, f32[512,256]{1,0:T(8,128)} %bitcast.35), custom_call_target="tpu_custom_call" | custom-call | tf_op jit(solution)/shard_map/cut/pallas_call | solution.py:433
  12.2 19.3 %all-to-all-start = ((f32[128,4,128]{2,1,0:T(4,128)}), f32[128,4,128]{2,1,0:T(4,128)S(1)}, u32[]{:S(2)}, u32[]{:S(2)}) async-start(f32[128,4,128]{2,1,0:T(4,128)} %bitcast.34), calls=%async_computation | async-start | bytes 524288 | tf_op jit(solution)/shard_map/all_to_all | solution.py:461
  31.5 0.0 collective-permute-done.4
  31.5 0.8 slice.25
  32.3 5.1 %collective-permute-start.6 = (f32[1024,128]{1,0:T(8,128)}, f32[1024,128]{1,0:T(8,128)}, u32[]{:S(2)}, u32[]{:S(2)}) collective-permute-start(f32[1024,128]{1,0:T(8,128)} %slice.25), channel_id=1, source_target_pairs={{0,3},{1,0},{2,1},{3,2},{4,7},{5,4},{6,5},{7,6},{8,11},{9,8},{10,9... | collective-permute-start | bytes 1572872 | tf_op jit(solution)/shard_map/ppermute | solution.py:394
  37.5 0.0 collective-permute-done.3
  37.5 0.8 slice.24
  38.3 1.9 %collective-permute-start.5 = (f32[1024,128]{1,0:T(8,128)}, f32[1024,128]{1,0:T(8,128)}, u32[]{:S(2)}, u32[]{:S(2)}) collective-permute-start(f32[1024,128]{1,0:T(8,128)} %slice.24), channel_id=1, source_target_pairs={{0,1},{1,2},{2,3},{3,0},{4,5},{5,6},{6,7},{7,4},{8,9},{9,10},{10,1... | collective-permute-start | bytes 1572872 | tf_op jit(solution)/shard_map/ppermute | solution.py:394
  40.2 0.0 copy-start.5
  40.2 5.9 %receivers.1.extra_hbm = f32[8192,128]{1,0:T(8,128)} custom-call(s32[1,512]{1,0:T(1,128)} %index_hbm.1, f32[3,1,512]{2,1,0:T(1,128)} %bitcast.40), custom_call_target="tpu_custom_call" | custom-call | tf_op jit(solution)/shard_map/receivers/pallas_call | solution.py:445
  46.1 7.3 %all-to-all-done = f32[128,4,128]{2,1,0:T(4,128)S(1)} async-done(((f32[128,4,128]{2,1,0:T(4,128)}), f32[128,4,128]{2,1,0:T(4,128)S(1)}, u32[]{:S(2)}, u32[]{:S(2)}) %all-to-all-start) | async-done | bytes 262176 | tf_op jit(solution)/shard_map/all_to_all | solution.py:461
  53.4 0.0 copy-start
  53.4 4.4 %collective-permute-start.2 = (f32[512,128]{1,0:T(8,128)S(1)}, f32[512,128]{1,0:T(8,128)S(1)}, u32[]{:S(2)}, u32[]{:S(2)}) collective-permute-start(f32[512,128]{1,0:T(8,128)S(1)} %bitcast.26), channel_id=1, source_target_pairs={{0,2},{1,3},{2,0},{3,1},{4,6},{5,7},{6,4},{7,5},{8,10},{9,11},{10,... | collective-permute-start | bytes 786440 | tf_op jit(solution)/shard_map/ppermute | solution.py:394
  57.8 3.0 %collective-permute-start.1 = (f32[512,128]{1,0:T(8,128)S(1)}, f32[512,128]{1,0:T(8,128)S(1)}, u32[]{:S(2)}, u32[]{:S(2)}) collective-permute-start(f32[512,128]{1,0:T(8,128)S(1)} %bitcast.27), channel_id=1, source_target_pairs={{0,3},{1,0},{2,1},{3,2},{4,7},{5,4},{6,5},{7,6},{8,11},{9,8},{10,9... | collective-permute-start | bytes 786440 | tf_op jit(solution)/shard_map/ppermute | solution.py:394
  60.9 2.8 %collective-permute-start = (f32[512,128]{1,0:T(8,128)S(1)}, f32[512,128]{1,0:T(8,128)S(1)}, u32[]{:S(2)}, u32[]{:S(2)}) collective-permute-start(f32[512,128]{1,0:T(8,128)S(1)} %bitcast.28), channel_id=1, source_target_pairs={{0,1},{1,2},{2,3},{3,0},{4,5},{5,6},{6,7},{7,4},{8,9},{9,10},{10,1... | collective-permute-start | bytes 786440 | tf_op jit(solution)/shard_map/ppermute | solution.py:394
  64.3 0.0 collective-permute-done.6
  64.4 0.0 collective-permute-done.5
  64.4 0.0 copy-done.1
  64.4 0.0 copy-done.2
  64.4 2.3 %before.1 = (f32[24,128,128]{2,1,0:T(8,128)S(1)}, f32[16,128,128]{2,1,0:T(8,128)S(1)}, f32[16,128,128]{2,1,0:T(8,128)S(1)}, f32[16,128,128]{2,1,0:T(8,128)S(1)}, f32[16,128,128]{2,1,0:T(8,128)S(1)}) custom-call(s32[1]{0:T(128)} %bitcast.me_ref, f32[16,128,128]{2,1,0:T(8,128)S(1)} %bitcast.23, f32[16,128,128]{2,1,0:T(8,128)S(1)} %bitcast.25, ...), custom_call_target="tpu_custom_call" | custom-call | tf_op jit(solution)/shard_map/before/pallas_call | solution.py:467
  66.7 0.0 collective-permute-done.2.far_ref
  66.7 4.9 %collective-permute-done.1.right_ref = f32[512,128]{1,0:T(8,128)S(1)} collective-permute-done((f32[512,128]{1,0:T(8,128)S(1)}, f32[512,128]{1,0:T(8,128)S(1)}, u32[]{:S(2)}, u32[]{:S(2)}) %collective-permute-start.1) | collective-permute-done | bytes 262176 | tf_op jit(solution)/shard_map/ppermute | solution.py:394
  71.6 0.3 collective-permute-done.left_ref
  71.9 0.0 copy-done.5
  71.9 0.0 copy-done
  71.9 0.0 copy-start.3
  71.9 0.0 copy-start.4
  71.9 5.7 %window.1 = (f32[512,128]{1,0:T(8,128)S(1)}, bf16[4,128,128]{2,1,0:T(8,128)(2,1)S(1)}, bf16[4,128,128]{2,1,0:T(8,128)(2,1)S(1)}) custom-call(s32[1]{0:T(128)} %bitcast.me_ref, s32[1]{0:T(128)S(6)} %copy.17.source_ref, f32[1,3]{1,0:T(1,128)S(1)} %copy-done.5, f32[512,128]{1,0:T(8,128)S(1)} %bitcast.29, f32[512,128]{1,0:T(8,128)S(1)} %collective-permute-done.left_ref, ...), custom_call_target="tpu_custom_call" | custom-call | tf_op jit(solution)/shard_map/window/pallas_call | solution.py:483
  77.6 34.0 %all_to_all.15 = f32[128,4,128]{2,1,0:T(4,128)S(1)} all-to-all(f32[128,4,128]{2,1,0:T(4,128)S(1)} %bitcast.31), channel_id=1, replica_groups=mesh['shots'=128,'sub'=4] {'shots'}, dimensions={0} | all-to-all | bytes 524288 | tf_op jit(solution)/shard_map/all_to_all | solution.py:511
  111.5 0.0 copy-done.3
  111.5 0.0 copy-done.4
  111.5 2.2 %spread.1 = f32[512,256]{1,0:T(8,128)} custom-call(s32[1]{0:T(128)} %bitcast.me_ref, s32[128]{0:T(128)S(1)} %copy-done.3, s32[128]{0:T(128)S(1)} %copy-done.4, f32[512,128]{1,0:T(8,128)S(1)} %bitcast.30), custom_call_target="tpu_custom_call" | custom-call | tf_op jit(solution)/shard_map/spread/pallas_call | solution.py:514
  113.7 3.5 %all-to-all-start.2 = ((f32[4,128,256]{2,1,0:T(8,128)}), f32[4,128,256]{2,1,0:T(8,128)S(1)}, u32[]{:S(2)}, u32[]{:S(2)}) async-start(f32[4,128,256]{2,1,0:T(8,128)} %bitcast.16), calls=%async_computation.2 | async-start | bytes 1048576 | tf_op jit(solution)/shard_map/all_to_all | solution.py:523
  117.2 0.8 copy.15
  118.0 0.8 copy.16
  118.7 8.5 %all-to-all-done.2 = f32[4,128,256]{2,1,0:T(8,128)S(1)} async-done(((f32[4,128,256]{2,1,0:T(8,128)}), f32[4,128,256]{2,1,0:T(8,128)S(1)}, u32[]{:S(2)}, u32[]{:S(2)}) %all-to-all-start.2) | async-done | bytes 524320 | tf_op jit(solution)/shard_map/all_to_all | solution.py:523
  127.2 0.7 slice_add_fusion
Async XLA Ops:
  3.1 61.3 %copy-start.1 = (f32[2048,128]{1,0:T(8,128)S(1)}, f32[2048,128]{1,0:T(8,128)}, u32[]{:S(2)}) copy-start(f32[2048,128]{1,0:T(8,128)} %fields.1) | copy-start | bytes 3145732
  3.1 61.3 %copy-start.2 = (bf16[128,128]{1,0:T(8,128)(2,1)S(1)}, bf16[128,128]{1,0:T(8,128)(2,1)}, u32[]{:S(2)}) copy-start(bf16[128,128]{1,0:T(8,128)(2,1)} %constant.6.clone.band_ref) | copy-start | bytes 98308
  3.1 28.4 %collective-permute-start.4 = (f32[2048,128]{1,0:T(8,128)}, f32[2048,128]{1,0:T(8,128)S(1)}, u32[]{:S(2)}, u32[]{:S(2)}) collective-permute-start(f32[2048,128]{1,0:T(8,128)} %fields.1), channel_id=1, source_target_pairs={{0,3},{1,0},{2,1},{3,2},{4,7},{5,4},{6,5},{7,6},{8,11},{9,8},{10,9... | collective-permute-start | bytes 3145736 | tf_op jit(solution)/shard_map/ppermute | solution.py:394
  7.9 29.6 %collective-permute-start.3 = (f32[2048,128]{1,0:T(8,128)}, f32[2048,128]{1,0:T(8,128)S(1)}, u32[]{:S(2)}, u32[]{:S(2)}) collective-permute-start(f32[2048,128]{1,0:T(8,128)} %fields.1), channel_id=1, source_target_pairs={{0,1},{1,2},{2,3},{3,0},{4,5},{5,6},{6,7},{7,4},{8,9},{9,10},{10,1... | collective-permute-start | bytes 3145736 | tf_op jit(solution)/shard_map/ppermute | solution.py:394
  12.2 41.2 %all-to-all-start = ((f32[128,4,128]{2,1,0:T(4,128)}), f32[128,4,128]{2,1,0:T(4,128)S(1)}, u32[]{:S(2)}, u32[]{:S(2)}) async-start(f32[128,4,128]{2,1,0:T(4,128)} %bitcast.34), calls=%async_computation | async-start | bytes 524288 | tf_op jit(solution)/shard_map/all_to_all | solution.py:461
  32.3 32.0 %collective-permute-start.6 = (f32[1024,128]{1,0:T(8,128)}, f32[1024,128]{1,0:T(8,128)}, u32[]{:S(2)}, u32[]{:S(2)}) collective-permute-start(f32[1024,128]{1,0:T(8,128)} %slice.25), channel_id=1, source_target_pairs={{0,3},{1,0},{2,1},{3,2},{4,7},{5,4},{6,5},{7,6},{8,11},{9,8},{10,9... | collective-permute-start | bytes 1572872 | tf_op jit(solution)/shard_map/ppermute | solution.py:394
  38.3 26.1 %collective-permute-start.5 = (f32[1024,128]{1,0:T(8,128)}, f32[1024,128]{1,0:T(8,128)}, u32[]{:S(2)}, u32[]{:S(2)}) collective-permute-start(f32[1024,128]{1,0:T(8,128)} %slice.24), channel_id=1, source_target_pairs={{0,1},{1,2},{2,3},{3,0},{4,5},{5,6},{6,7},{7,4},{8,9},{9,10},{10,1... | collective-permute-start | bytes 1572872 | tf_op jit(solution)/shard_map/ppermute | solution.py:394
  40.2 31.7 %copy-start.5 = (f32[1,3]{1,0:T(1,128)S(1)}, f32[1,3]{1,0:T(1,128)}, u32[]{:S(2)}) copy-start(f32[1,3]{1,0:T(1,128)} %wave_ref.1) | copy-start | bytes 40
  53.4 18.5 %copy-start = (f32[8192,128]{1,0:T(8,128)S(1)}, f32[8192,128]{1,0:T(8,128)}, u32[]{:S(2)}) copy-start(f32[8192,128]{1,0:T(8,128)} %receivers.1.extra_hbm) | copy-start | bytes 12582916
  53.4 13.3 %collective-permute-start.2 = (f32[512,128]{1,0:T(8,128)S(1)}, f32[512,128]{1,0:T(8,128)S(1)}, u32[]{:S(2)}, u32[]{:S(2)}) collective-permute-start(f32[512,128]{1,0:T(8,128)S(1)} %bitcast.26), channel_id=1, source_target_pairs={{0,2},{1,3},{2,0},{3,1},{4,6},{5,7},{6,4},{7,5},{8,10},{9,11},{10,... | collective-permute-start | bytes 786440 | tf_op jit(solution)/shard_map/ppermute | solution.py:394
  57.8 13.7 %collective-permute-start.1 = (f32[512,128]{1,0:T(8,128)S(1)}, f32[512,128]{1,0:T(8,128)S(1)}, u32[]{:S(2)}, u32[]{:S(2)}) collective-permute-start(f32[512,128]{1,0:T(8,128)S(1)} %bitcast.27), channel_id=1, source_target_pairs={{0,3},{1,0},{2,1},{3,2},{4,7},{5,4},{6,5},{7,6},{8,11},{9,8},{10,9... | collective-permute-start | bytes 786440 | tf_op jit(solution)/shard_map/ppermute | solution.py:394
  60.9 11.0 %collective-permute-start = (f32[512,128]{1,0:T(8,128)S(1)}, f32[512,128]{1,0:T(8,128)S(1)}, u32[]{:S(2)}, u32[]{:S(2)}) collective-permute-start(f32[512,128]{1,0:T(8,128)S(1)} %bitcast.28), channel_id=1, source_target_pairs={{0,1},{1,2},{2,3},{3,0},{4,5},{5,6},{6,7},{7,4},{8,9},{9,10},{10,1... | collective-permute-start | bytes 786440 | tf_op jit(solution)/shard_map/ppermute | solution.py:394
  71.9 39.7 %copy-start.3 = (s32[128]{0:T(128)S(1)}, s32[128]{0:T(128)}, u32[]{:S(2)}) copy-start(s32[128]{0:T(128)} %ax_ref.1) | copy-start | bytes 1540
  71.9 39.7 %copy-start.4 = (s32[128]{0:T(128)S(1)}, s32[128]{0:T(128)}, u32[]{:S(2)}) copy-start(s32[128]{0:T(128)} %ay_ref.1) | copy-start | bytes 1540
  113.7 13.5 %all-to-all-start.2 = ((f32[4,128,256]{2,1,0:T(8,128)}), f32[4,128,256]{2,1,0:T(8,128)S(1)}, u32[]{:S(2)}, u32[]{:S(2)}) async-start(f32[4,128,256]{2,1,0:T(8,128)} %bitcast.16), calls=%async_computation.2 | async-start | bytes 1048576 | tf_op jit(solution)/shard_map/all_to_all | solution.py:523
